TPU v7x, 256 devices: a whole 4x4x8 slice. The times are simulated.
256 devices in a mesh: ctx: 64 (over x, z_hi, y), ch: 4 (over z_lo, core).
Axes of the slice: x: 4, y: 4, z: 8 (z_hi: 4, z_lo: 2; z = z_hi * 2 + z_lo), core: 2. Of those that a mesh axis runs over, the one named last changes fastest.
Arguments:
- tokens: int32 [8192], P('ctx'), may hold values from 0 to 511
- complement: int32 [512], replicated, may hold values from 0 to 511, each once
- seg_lengths: int32 [256], replicated, may hold values from 1 to 256, as said below
- owner: int32 [64], replicated, may hold values from 0 to 63, each once
- embed: bfloat16 [512, 4096], P(None, 'ch')
- norm_gain: float32 [4096], P('ch'), may hold values from 0.24 to 10.3
- taps: float32 [128, 4096], P(None, 'ch'), may hold values from -0.54 to 0.54
- w_out: bfloat16 [4096, 4096], P('ch', 'ctx'), may hold values from -2 to 2
Outputs:
- owned: float32 [256, 4096], P('ctx', 'ch')
Inputs may be any that keep to these rules, and one draw needn't show every extreme that they name: `seg_lengths`: segment lengths sum to 8192; the first segment is exactly 256 long and no segment is longer. `complement`: a permutation of the token ids. `owner`: a permutation of the ctx indices.
All inputs are finite; a program needn't handle non-finite values.
Results may differ from a plain program's by a relative error of at most 0.0023.
Values may be sent and summed in bfloat16 or wider, within the bound.
A program may use at most 128 MiB of HBM per device.

v0:
```python
import functools

import jax
import jax.numpy as jnp
from jax import lax
from jax.experimental import pallas as pl
from jax.experimental.pallas import tpu as pltpu
from jax.sharding import PartitionSpec as P

norm_eps = 1e-06
LANES = 128
SUB = 8


def passed_along(array, axis, by):
    peers = lax.axis_size(axis)
    pairs = [(i, i + by) for i in range(peers) if 0 <= i + by < peers]
    return lax.ppermute(array, axis, pairs)


def mix_kernel(tok_ref, comp_ref, start_ref, end_ref, embed_ref, inv_ref, gain_ref, taps_ref,
               out_ref, tab, ext_f, ext_r, taps_v, res):
    vocab, width = embed_ref.shape
    count = out_ref.shape[0]
    span = taps_ref.shape[0]
    blocks = count // SUB
    for s in range(SUB):
        cols = slice(s * LANES, (s + 1) * LANES)
        rows = embed_ref[:, cols].astype(jnp.float32) * inv_ref[...] * gain_ref[:, cols]
        tab[pl.ds(s, vocab, stride=SUB), :] = rows.astype(jnp.bfloat16).astype(jnp.float32)
        taps_v[pl.ds(s, span, stride=SUB), :] = taps_ref[:, cols]
    taps_v[pl.ds(span * SUB, SUB * SUB), :] = jnp.zeros((SUB * SUB, LANES), jnp.float32)

    def row_of(ref, k):
        return ref[pl.ds(pl.multiple_of(k * SUB, SUB), SUB), :]

    def put(ref, k, v):
        ref[pl.ds(pl.multiple_of(k * SUB, SUB), SUB), :] = v

    def fill(k8, carry):
        for u in range(SUB):
            k = k8 * SUB + u
            put(ext_f, k, row_of(tab, tok_ref[k]))
            put(ext_r, k, row_of(tab, comp_ref[tok_ref[count + k]]))
        return carry

    lax.fori_loop(0, 2 * count // SUB, fill, 0)

    def tree(terms):
        while len(terms) > 1:
            terms = [a + b for a, b in zip(terms[::2], terms[1::2])] + (
                [terms[-1]] if len(terms) % 2 else []
            )
        return terms[0]

    zero = jnp.zeros((SUB, LANES), jnp.float32)

    def block(i, carry):
        p0 = i * SUB
        s0 = start_ref[p0]
        e0 = end_ref[p0 + SUB - 1]

        def fwd_far(j, acc):
            q0 = j * SUB
            lag = (i - j) * SUB
            rows = [jnp.where(q0 + c >= s0, row_of(ext_f, count + q0 + c), zero) for c in range(SUB)]
            tap = {d: row_of(taps_v, lag + d) for d in range(1 - SUB, SUB)}
            return tuple(
                acc[r] + tree([tap[r - c] * rows[c] for c in range(SUB)]) for r in range(SUB)
            )

        low = jnp.maximum(lax.div(s0 + count, SUB) - blocks, i - span // SUB)
        far_f = lax.fori_loop(low, i, fwd_far, (zero,) * SUB)

        def rev_far(j, acc):
            q0 = j * SUB
            lag = (j - i) * SUB
            rows = [jnp.where(q0 + c < e0, row_of(ext_r, q0 + c), zero) for c in range(SUB)]
            tap = {d: row_of(taps_v, lag + d) for d in range(1 - SUB, SUB)}
            return tuple(
                acc[r] + tree([tap[c - r] * rows[c] for c in range(SUB)]) for r in range(SUB)
            )

        high = jnp.minimum(lax.div(e0 - 1, SUB), i + span // SUB)
        far_r = lax.fori_loop(i + 1, high + 1, rev_far, (zero,) * SUB)

        rows_f = [row_of(ext_f, count + p0 + c) for c in range(SUB)]
        rows_r = [row_of(ext_r, p0 + c) for c in range(SUB)]
        tap = [row_of(taps_v, d) for d in range(SUB)]
        for r in range(SUB):
            start = start_ref[p0 + r]
            end = end_ref[p0 + r]
            terms = [tap[0] * rows_f[r], jnp.where(start < p0, far_f[r], zero)]
            terms += [jnp.where(start <= p0 + c, tap[r - c] * rows_f[c], zero) for c in range(r)]
            gated_f = (rows_f[r] * tree(terms)).astype(jnp.bfloat16).astype(jnp.float32)
            terms = [tap[0] * rows_r[r], jnp.where(end > p0 + SUB, far_r[r], zero)]
            terms += [
                jnp.where(end > p0 + c, tap[c - r] * rows_r[c], zero) for c in range(r + 1, SUB)
            ]
            gated_r = (rows_r[r] * tree(terms)).astype(jnp.bfloat16).astype(jnp.float32)
            put(res, p0 + r, (gated_f + gated_r) * 0.5)
        return carry

    lax.fori_loop(0, blocks, block, 0)
    for s in range(SUB):
        out_ref[:, s * LANES : (s + 1) * LANES] = res[pl.ds(s, count, stride=SUB), :].astype(
            jnp.bfloat16
        )


def mix_strands(tok_ext, complement, starts, ends, embed, inv, gain, taps):
    vocab, width = embed.shape
    count = starts.shape[0]
    span = taps.shape[0]
    smem = pl.BlockSpec(memory_space=pltpu.SMEM)
    vmem = pl.BlockSpec(memory_space=pltpu.VMEM)
    return pl.pallas_call(
        mix_kernel,
        out_shape=jax.ShapeDtypeStruct((count, width), jnp.bfloat16),
        in_specs=[smem] * 4 + [vmem] * 4,
        out_specs=vmem,
        scratch_shapes=[
            pltpu.VMEM((vocab * SUB, LANES), jnp.float32),
            pltpu.VMEM((2 * count * SUB, LANES), jnp.float32),
            pltpu.VMEM((2 * count * SUB, LANES), jnp.float32),
            pltpu.VMEM(((span + SUB) * SUB, LANES), jnp.float32),
            pltpu.VMEM((count * SUB, LANES), jnp.float32),
        ],
        compiler_params=pltpu.CompilerParams(vmem_limit_bytes=32 << 20),
        cost_estimate=pl.CostEstimate(flops=2 * 2 * count * span * width, bytes_accessed=4 << 20, transcendentals=0),
    )(tok_ext, complement, starts, ends, embed, inv, gain, taps)


def body(tokens, complement, seg_lengths, owner, embed, norm_gain, taps, w_out):
    row_count = tokens.shape[0]
    vocab_size, width = embed.shape
    ctx_count = lax.axis_size("ctx")
    ch_count = lax.axis_size("ch")
    place = lax.axis_index("ctx")
    full_width = width * ch_count
    seg_count = seg_lengths.shape[0]
    block_total = owner.shape[0]
    per_block = seg_count // block_total
    near = 4
    far = ctx_count // near
    near_groups = [[near * m + y for y in range(near)] for m in range(far)]
    far_groups = [[near * m + y for m in range(far)] for y in range(near)]
    out_cols = w_out.shape[1]

    w_rows = lax.all_gather(
        w_out.T, "ctx", axis=0, tiled=True, axis_index_groups=far_groups
    )

    power = lax.psum(jnp.sum(jnp.square(embed.astype(jnp.float32)), axis=1), "ch")
    inv = lax.rsqrt(power / full_width + norm_eps)[:, None]

    seg_ids = jnp.arange(seg_count, dtype=jnp.int32)
    seg_ends = jnp.sum(
        jnp.where(seg_ids[None, :] <= seg_ids[:, None], seg_lengths[None, :], 0), axis=1
    )
    seg_starts = seg_ends - seg_lengths
    own_pos = place * row_count + jnp.arange(row_count, dtype=jnp.int32)
    inside = (seg_starts[None, :] <= own_pos[:, None]) & (own_pos[:, None] < seg_ends[None, :])
    first_pos = jnp.sum(jnp.where(inside, seg_starts[None, :], 0), axis=1)
    end_pos = jnp.sum(jnp.where(inside, seg_ends[None, :], 0), axis=1)
    base = place * row_count
    starts = jnp.maximum(first_pos - base, -row_count)
    ends = jnp.minimum(end_pos - base, 2 * row_count)

    tok_ext = jnp.concatenate(
        [passed_along(tokens, "ctx", 1), tokens, passed_along(tokens, "ctx", -1)]
    )
    strand_mean = mix_strands(
        tok_ext, complement, starts, ends, embed, inv, norm_gain[None, :], taps
    )
    rows = lax.all_gather(
        strand_mean, "ctx", axis=0, tiled=True, axis_index_groups=near_groups
    )
    terms = lax.dot_general(
        rows, w_rows, (((1,), (1,)), ((), ())), preferred_element_type=jnp.float32
    )
    col_share = lax.psum_scatter(terms, "ch", scatter_dimension=1, tiled=True)
    active = jax.nn.softplus(col_share)

    slots = jnp.arange(seg_count, dtype=jnp.int32)
    block_ids = jnp.arange(block_total, dtype=jnp.int32)
    holder = jnp.sum(
        jnp.where(owner[None, :] == (slots // per_block)[:, None], block_ids[None, :], 0), axis=1
    )
    seg_at = holder * per_block + slots % per_block
    same_seg = seg_at[:, None] == slots[None, :]
    slot_start = jnp.sum(jnp.where(same_seg, seg_starts[None, :], 0), axis=1)
    slot_end = jnp.sum(jnp.where(same_seg, seg_ends[None, :], 0), axis=1)
    group_pos = (place // near) * (near * row_count) + jnp.arange(near * row_count, dtype=jnp.int32)
    member = (
        (slot_start[:, None] <= group_pos[None, :]) & (group_pos[None, :] < slot_end[:, None])
    ).astype(jnp.float32)
    partial_sums = jnp.dot(member, active, precision=lax.Precision.HIGHEST)
    share = partial_sums.shape[1]
    received = lax.all_to_all(
        partial_sums.reshape(ctx_count, per_block, share),
        "ctx",
        split_axis=0,
        concat_axis=0,
        tiled=True,
    )
    sums = jnp.sum(received.reshape(far, near, per_block, share), axis=0)
    sums = sums.reshape(near, per_block, far // ch_count, out_cols)
    totals = sums.transpose(1, 2, 0, 3).reshape(per_block, width)
    own_lengths = lax.dynamic_slice_in_dim(slot_end - slot_start, place * per_block, per_block)
    return totals / own_lengths.astype(jnp.float32)[:, None]


def solution(mesh):
    in_specs = (P("ctx"), P(), P(), P(), P(None, "ch"), P("ch"), P(None, "ch"), P("ch", "ctx"))
    out_specs = P("ctx", "ch")
    return jax.shard_map(body, mesh=mesh, in_specs=in_specs, out_specs=out_specs, check_vma=False)
```

profile of v0, /device:TPU:1, one launch (start us, length us, event | category | flops | bytes accessed | tf_op | source)
XLA Modules:
  0.0 205.8 jit_solution(17707992447096254528)
XLA Ops:
  6.5 1.3 collective-permute-start.1
  7.8 4.7 %collective-permute-start = (s32[128]{0:T(128)}, s32[128]{0:T(128)S(1)}, u32[]{:S(2)}, u32[]{:S(2)}) collective-permute-start(s32[128]{0:T(128)} %param.8), channel_id=1, source_target_pairs={{0,4},{4,8},{8,12},{12,16},{16,20},{20,24},{24,28},{28,32},{32,36}... | collective-permute-start | bytes 1544 | tf_op jit(solution)/shard_map/ppermute | solution.py:18
  12.5 0.8 select_reduce_fusion.2
  13.3 0.7 sub.25
  14.0 1.5 multiply_reduce_fusion
  15.5 8.1 %psum.7 = f32[512]{0:T(512)S(1)} all-reduce(f32[512]{0:T(512)S(1)} %multiply_reduce_fusion), channel_id=1, replica_groups=mesh['ctx'=64,'ch'=4] {'ch'}, use_global_device_ids=true, to_apply=%region_7.8 | all-reduce | flops 512 | bytes 4096 | tf_op jit(solution)/shard_map/psum | solution.py:154
  24.0 0.7 pad_add_fusion.tok_ref
  24.7 1.2 copy-done
  25.9 1.0 copy-done.1
  26.9 0.7 copy-done.2
  27.6 0.7 copy-done.3
  28.3 16.7 %shard_map.82 = bf16[128,1024]{1,0:T(8,128)(2,1)} custom-call(s32[384]{0:T(512)S(1)} %pad_add_fusion.tok_ref, s32[512]{0:T(512)S(1)} %copy-done.3, s32[128]{0:T(128)S(1)} %get-tuple-element.10.start_ref, s32[128]{0:T(128)S(1)} %get-tuple-element.9.end_ref, bf16[512,1024]{1,0:T(8,128)(2,1)S(1)} %copy-done, f32[512,1]{1,0:T(8,128)S(1)} %copy.12.inv_ref, ...), custom_call_target="tpu_custom_call" | custom-call | flops 67108864 | bytes 4194304 | tf_op jit(solution)/shard_map/pallas_call | solution.py:117
  45.1 0.7 all-gather.5.cloned.1.call-update
  45.8 28.3 %all-gather.3.cloned.1.call-done = bf16[512,1024]{1,0:T(8,128)(2,1)} async-done(((bf16[128,1024]{1,0:T(8,128)(2,1)}), bf16[512,1024]{1,0:T(8,128)(2,1)}) %all-gather.3.cloned.1.call-update) | async-done | bytes 1048592 | tf_op jit(solution)/shard_map/all_gather | solution.py:176
  74.1 62.8 %all-gather.5.cloned.1.call-done = bf16[1024,1024]{1,0:T(8,128)(2,1)} async-done(((bf16[64,1024]{1,0:T(8,128)(2,1)}), bf16[1024,1024]{1,0:T(8,128)(2,1)}) %all-gather.5.cloned.1.call-update) | async-done | bytes 2097168 | tf_op jit(solution)/shard_map/all_gather | solution.py:150
  136.9 4.5 %fusion.18 = f32[512,1024]{1,0:T(8,128)} fusion(bf16[512,1024]{1,0:T(8,128)(2,1)} %all-gather.3.cloned.1.call-done, bf16[1024,1024]{1,0:T(8,128)(2,1)} %all-gather.5.cloned.1.call-done), kind=kOutput, calls=%fused_computation.42 | convolution fusion | flops 1073741824 | bytes 5242880 | tf_op jit(solution)/shard_map/dot_general | solution.py:179
  141.5 0.6 copy-done.4
  142.2 0.2 select_reduce_fusion.1
  142.4 28.5 %reduce-scatter.2.cloned.1.call-done = f32[512,256]{1,0:T(8,128)} async-done(((f32[512,1024]{1,0:T(8,128)}), f32[512,256]{1,0:T(8,128)}) %reduce-scatter.2.cloned.1.call-update) | async-done | bytes 524304 | tf_op jit(solution)/shard_map/reduce_scatter | solution.py:182
  171.0 1.8 fusion
  172.8 0.8 reshape.53
  173.5 11.7 %all-to-all-start = ((f32[64,4,256]{2,1,0:T(4,128)}), f32[64,4,256]{2,1,0:T(4,128)S(1)}, u32[]{:S(2)}, u32[]{:S(2)}) async-start(f32[64,4,256]{2,1,0:T(4,128)} %reshape.53), calls=%async_computation.1 | async-start | bytes 524288 | tf_op jit(solution)/shard_map/all_to_all | solution.py:200
  185.4 13.0 %all-to-all-done = f32[64,4,256]{2,1,0:T(4,128)S(1)} async-done(((f32[64,4,256]{2,1,0:T(4,128)}), f32[64,4,256]{2,1,0:T(4,128)S(1)}, u32[]{:S(2)}, u32[]{:S(2)}) %all-to-all-start) | async-done | bytes 262176 | tf_op jit(solution)/shard_map/all_to_all | solution.py:200
  198.6 0.7 broadcast_divide_fusion
  (27 shorter events, 0.9 us)
Async XLA Ops:
  6.5 67.6 %all-gather.3.cloned.1.call-start = ((), (), s32[]{:S(2)}) async-start(), calls=%async_computation.2 | async-start | bytes 1310720 | tf_op jit(solution)/shard_map/all_gather | solution.py:176
  6.5 17.5 %collective-permute-start.1 = (s32[128]{0:T(128)}, s32[128]{0:T(128)S(1)}, u32[]{:S(2)}, u32[]{:S(2)}) collective-permute-start(s32[128]{0:T(128)} %param.8), channel_id=1, source_target_pairs={{4,0},{8,4},{12,8},{16,12},{20,16},{24,20},{28,24},{32,28},{36,32}... | collective-permute-start | bytes 1544 | tf_op jit(solution)/shard_map/ppermute | solution.py:18
  7.8 16.2 %collective-permute-start = (s32[128]{0:T(128)}, s32[128]{0:T(128)S(1)}, u32[]{:S(2)}, u32[]{:S(2)}) collective-permute-start(s32[128]{0:T(128)} %param.8), channel_id=1, source_target_pairs={{0,4},{4,8},{8,12},{12,16},{16,20},{20,24},{24,28},{28,32},{32,36}... | collective-permute-start | bytes 1544 | tf_op jit(solution)/shard_map/ppermute | solution.py:18
  24.7 1.2 copy-start
  25.9 1.0 copy-start.1
  26.9 0.7 copy-start.2
  27.6 0.7 copy-start.3
  45.0 91.9 %all-gather.5.cloned.1.call-start = ((), (), s32[]{:S(2)}) async-start(), calls=%async_computation.3 | async-start | bytes 2228224 | tf_op jit(solution)/shard_map/all_gather | solution.py:150
  45.8 125.2 %reduce-scatter.2.cloned.1.call-start = ((), (), s32[]{:S(2)}) async-start(), calls=%async_computation.4 | async-start | bytes 2621440 | tf_op jit(solution)/shard_map/reduce_scatter | solution.py:182
  141.4 0.7 copy-start.4
  173.5 24.8 %all-to-all-start = ((f32[64,4,256]{2,1,0:T(4,128)}), f32[64,4,256]{2,1,0:T(4,128)S(1)}, u32[]{:S(2)}, u32[]{:S(2)}) async-start(f32[64,4,256]{2,1,0:T(4,128)} %reshape.53), calls=%async_computation.1 | async-start | bytes 524288 | tf_op jit(solution)/shard_map/all_to_all | solution.py:200
Sparse Core Ops, SparseCore 0:
  45.1 28.9 all-gather.2
  76.5 60.3 all-gather.4
  141.6 29.3 reduce-scatter.1
where the time goes:
time: 207 us; the launch traced here: 206 us
  waiting for transfers between devices  133 us (64%)
  starting transfers between devices  17.7 us (9%)
  Pallas kernels  16.7 us (8%)
  between operations  13.2 us (6%)
  blocking collectives  8.14 us (4%)
  matrix products  6.29 us (3%)
  local copies, waits for them, and re-layouts  5.33 us (3%)
  other arithmetic  5 us (2%)
    all_gather x1, waiting for transfers between devices, body(): lax.all_gather(w_out.T, 'ctx', axis=0, tiled=True, axis_index_groups=far_...  62.8 us
    reduce_scatter x1, waiting for transfers between devices, body(): col_share = lax.psum_scatter(terms, 'ch', scatter_dimension=1, tiled=True)  28.5 us
    all_gather x1, waiting for transfers between devices, body(): lax.all_gather(strand_mean, 'ctx', axis=0, tiled=True, axis_index_groups=...  28.3 us
    pallas_call x1, Pallas kernels, mix_strands(): pl.pallas_call(mix_kernel, out_shape=jax.ShapeDtypeStruct((count, width),...  16.7 us
    all_to_all x1, waiting for transfers between devices, body(): lax.all_to_all(partial_sums.reshape(ctx_count, per_block, share), 'ctx',...  13 us
    all_to_all x1, starting transfers between devices, body(): lax.all_to_all(partial_sums.reshape(ctx_count, per_block, share), 'ctx',...  11.7 us
    psum x1, blocking collectives, body(): lax.psum(jnp.sum(jnp.square(embed.astype(jnp.float32)), axis=1), 'ch')  8.14 us
    ppermute x2, starting transfers between devices, passed_along(): return lax.ppermute(array, axis, pairs)  5.94 us
  transfers between devices with their start and end apart: 6, of which 4 were waited for; matrix products, arithmetic and copies ran while one was open for 2% of the time, Pallas kernels for 0%

commit v1 on v0

--- a/solution.py
+++ b/solution.py
@@ -1,5 +1,3 @@
-import functools
-
 import jax
 import jax.numpy as jnp
 from jax import lax
@@ -10,6 +8,7 @@
 norm_eps = 1e-06
 LANES = 128
 SUB = 8
+MESH = pl.DeviceIdType.MESH
 
 
 def passed_along(array, axis, by):
@@ -131,10 +130,285 @@
     )(tok_ext, complement, starts, ends, embed, inv, gain, taps)
 
 
+def exchange_kernel(s_ref, w_ref, member_ref, out_ref,
+                    sbuf, wbuf, out1, in1, zout, zin, pbuf, rbuf,
+                    w_send, w_recv, s_send, s_recv, r_send, r_recv, a_send, a_recv):
+    me = lax.axis_index("ctx")
+    ch = lax.axis_index("ch")
+    peers = lax.axis_size("ctx")
+    y = lax.rem(me, 4)
+    zh = lax.rem(lax.div(me, 4), 4)
+    x = lax.div(me, 16)
+    zl = lax.div(ch, 2)
+    core = lax.rem(ch, 2)
+
+    def ring(v, by):
+        return lax.rem(v + by, 4)
+
+    xp, xm, x2 = ring(x, 1), ring(x, 3), ring(x, 2)
+    zp, zm, z2 = ring(zh, 1), ring(zh, 3), ring(zh, 2)
+    yp, ym, y2 = ring(y, 1), ring(y, 3), ring(y, 2)
+    core_peer = zl * 2 + 1 - core
+    z_peer = (1 - zl) * 2 + core
+
+    barrier = pltpu.get_barrier_semaphore()
+
+    def hello(d, carry):
+        pl.semaphore_signal(
+            barrier, inc=1, device_id={"ctx": lax.rem(me + d, peers)}, device_id_type=MESH
+        )
+        return carry
+
+    lax.fori_loop(1, peers, hello, 0)
+    for other in (core_peer, z_peer):
+        pl.semaphore_signal(barrier, inc=1, device_id={"ch": other}, device_id_type=MESH)
+    pl.semaphore_wait(barrier, peers + 1)
+
+    cols = w_ref.shape[0]
+    half = cols // 2
+    rows = s_ref.shape[0]
+    parts = 4
+    chunk = rows // parts
+
+    def at_ctx(cx, cz, cy):
+        return {"ctx": cx * 16 + cz * 4 + cy}
+
+    def w_rows(cx, cz, lo=0, count=cols):
+        return wbuf.at[pl.ds(pl.multiple_of((cx * 4 + cz) * cols + lo, half), count), :]
+
+    def w_copy(label, src, dst, to):
+        return pltpu.make_async_remote_copy(
+            src_ref=src, dst_ref=dst, send_sem=w_send.at[label], recv_sem=w_recv.at[label],
+            device_id=to, device_id_type=MESH,
+        )
+
+    z_of = (zh, zm, zp, z2)
+    plus, minus = at_ctx(xp, zh, y), at_ctx(xm, zh, y)
+    up, down = at_ctx(x, zp, y), at_ctx(x, zm, y)
+    own = w_rows(x, zh)
+    sent = {
+        0: (w_ref, own, up),
+        1: (w_ref, own, down),
+        2: (w_rows(x, zm, 0, half), w_rows(x, zm, 0, half), up),
+        3: (w_rows(x, zp, half, half), w_rows(x, zp, half, half), down),
+    }
+    got = {
+        0: w_rows(x, zm),
+        1: w_rows(x, zp),
+        2: w_rows(x, z2, 0, half),
+        3: w_rows(x, z2, half, half),
+    }
+    for dz in range(4):
+        base = 4 + 3 * dz
+        here = w_rows(x, z_of[dz])
+        src = w_ref if dz == 0 else here
+        sent[base] = (src, here, plus)
+        sent[base + 1] = (src, here, minus)
+        relay = w_rows(xm if dz < 2 else xp, z_of[dz])
+        sent[base + 2] = (relay, relay, plus if dz < 2 else minus)
+        got[base] = w_rows(xm, z_of[dz])
+        got[base + 1] = w_rows(xp, z_of[dz])
+        got[base + 2] = w_rows(x2, z_of[dz])
+
+    def w_start(*labels):
+        for n in labels:
+            w_copy(n, *sent[n]).start()
+
+    def w_wait(*labels):
+        for n in labels:
+            w_copy(n, got[n], got[n], plus).wait_recv()
+
+    def s_rows(cy, k):
+        return sbuf.at[pl.ds(pl.multiple_of(cy * rows + k * chunk, chunk), chunk), :]
+
+    s_plus, s_minus = at_ctx(x, zh, yp), at_ctx(x, zh, ym)
+
+    def s_copy(k, kind, src, dst, to):
+        return pltpu.make_async_remote_copy(
+            src_ref=src, dst_ref=dst, send_sem=s_send.at[3 * k + kind],
+            recv_sem=s_recv.at[3 * k + kind], device_id=to, device_id_type=MESH,
+        )
+
+    def s_sent(k, kind):
+        if kind < 2:
+            return s_copy(
+                k, kind, s_ref.at[pl.ds(k * chunk, chunk), :], s_rows(y, k),
+                s_plus if kind == 0 else s_minus,
+            )
+        relay = s_rows(ym if k % 2 == 0 else yp, k)
+        return s_copy(k, kind, relay, relay, s_plus if k % 2 == 0 else s_minus)
+
+    def s_wait(k, kind):
+        there = s_rows((ym, yp, y2)[kind], k)
+        s_copy(k, kind, there, there, s_plus).wait_recv()
+
+    w_start(0, 1, 4, 5)
+    for k in range(parts):
+        s_sent(k, 0).start()
+        s_sent(k, 1).start()
+    wbuf[pl.ds(pl.multiple_of((x * 4 + zh) * cols, cols), cols), :] = w_ref[...]
+    sbuf[pl.ds(pl.multiple_of(y * rows, rows), rows), :] = s_ref[...]
+    w_wait(0)
+    w_start(2, 7, 8)
+    w_wait(1)
+    w_start(3, 10, 11)
+    w_wait(4)
+    w_start(6)
+    for k in range(parts):
+        s_wait(k, k % 2)
+        s_sent(k, 2).start()
+    w_wait(2, 3)
+    w_start(13, 14)
+    w_wait(7)
+    w_start(9)
+    w_wait(11)
+    w_start(12)
+    w_wait(14)
+    w_start(15)
+    for k in range(parts):
+        s_wait(k, 1 - k % 2)
+        s_wait(k, 2)
+    w_wait(5, 6, 8, 9, 10, 12, 13, 15)
+
+    group = 4 * cols
+    total = parts * rows
+    tile = rows
+
+    def product(g, t):
+        lhs = sbuf[pl.ds(pl.multiple_of(t * tile, tile), tile), :]
+        rhs = wbuf[pl.ds(pl.multiple_of(g * group, group), group), :]
+        return lax.dot_general(
+            lhs, rhs, (((1,), (1,)), ((), ())), preferred_element_type=jnp.float32
+        )
+
+    def tile_of(ref, *lead, t):
+        return ref.at[(*lead, pl.ds(pl.multiple_of(t * tile, tile), tile), slice(None))]
+
+    def core_copy(slot):
+        return pltpu.make_async_remote_copy(
+            src_ref=out1.at[slot], dst_ref=in1.at[slot], send_sem=r_send.at[slot],
+            recv_sem=r_recv.at[slot], device_id={"ch": core_peer}, device_id_type=MESH,
+        )
+
+    z_copy = pltpu.make_async_remote_copy(
+        src_ref=zout, dst_ref=zin, send_sem=r_send.at[2], recv_sem=r_recv.at[2],
+        device_id={"ch": z_peer}, device_id_type=MESH,
+    )
+    for slot, g in ((0, 2 * (1 - zl) + 1 - core), (1, 2 * zl + 1 - core)):
+        def give(t, carry, slot=slot, g=g):
+            tile_of(out1, slot, t=t)[...] = product(g, t)
+            return carry
+
+        lax.fori_loop(0, total // tile, give, 0)
+        core_copy(slot).start()
+    core_copy(0).wait_recv()
+
+    def pass_on(t, carry):
+        summed = product(2 * (1 - zl) + core, t) + tile_of(in1, 0, t=t)[...]
+        tile_of(zout, t=t)[...] = summed.astype(jnp.bfloat16)
+        return carry
+
+    lax.fori_loop(0, total // tile, pass_on, 0)
+    z_copy.start()
+    core_copy(1).wait_recv()
+
+    def keep(t, carry):
+        ref = tile_of(in1, 1, t=t)
+        ref[...] = product(2 * zl + core, t) + ref[...]
+        return carry
+
+    lax.fori_loop(0, total // tile, keep, 0)
+    z_copy.wait_recv()
+
+    def sum_up(t, acc):
+        scores = tile_of(in1, 1, t=t)[...] + tile_of(zin, t=t)[...].astype(jnp.float32)
+        active = jnp.maximum(scores, 0.0) + jnp.log1p(jnp.exp(-jnp.abs(scores)))
+        high = active.astype(jnp.bfloat16)
+        low = (active - high.astype(jnp.float32)).astype(jnp.bfloat16)
+        picks = member_ref[t]
+        return (
+            acc
+            + jnp.dot(picks, high, preferred_element_type=jnp.float32)
+            + jnp.dot(picks, low, preferred_element_type=jnp.float32)
+        )
+
+    slots = member_ref.shape[1]
+    sums = lax.fori_loop(0, total // tile, sum_up, jnp.zeros((slots, group), jnp.float32))
+    wide = group // LANES
+    for h in range(wide):
+        pbuf[pl.ds(h, slots, stride=wide), :] = sums[:, h * LANES : (h + 1) * LANES]
+
+    def to_owner(d, carry):
+        dest = lax.rem(me + d, peers)
+        pltpu.make_async_remote_copy(
+            src_ref=pbuf.at[pl.ds(pl.multiple_of(dest * SUB, SUB), SUB), :],
+            dst_ref=rbuf.at[pl.ds(pl.multiple_of(me * SUB, SUB), SUB), :],
+            send_sem=a_send, recv_sem=a_recv, device_id={"ctx": dest}, device_id_type=MESH,
+        ).start()
+        return carry
+
+    lax.fori_loop(1, peers, to_owner, 0)
+    mine = pl.ds(pl.multiple_of(me * SUB, SUB), SUB)
+    rbuf[mine, :] = pbuf[mine, :]
+    most = pl.ds(0, (peers - 1) * SUB)
+    all_of = pltpu.make_async_remote_copy(
+        src_ref=pbuf.at[most, :], dst_ref=rbuf.at[most, :], send_sem=a_send, recv_sem=a_recv,
+        device_id={"ctx": lax.rem(me + 1, peers)}, device_id_type=MESH,
+    )
+    all_of.wait_recv()
+    for q in range(4):
+        acc = rbuf[pl.ds(q * SUB, SUB), :]
+        for m in range(1, peers // 4):
+            acc = acc + rbuf[pl.ds((4 * m + q) * SUB, SUB), :]
+        out_ref[pl.ds(q * SUB, SUB), :] = acc
+    all_of.wait_send()
+    for n in range(16):
+        w_copy(n, *sent[n]).wait_send()
+    for k in range(parts):
+        for kind in range(3):
+            s_sent(k, kind).wait_send()
+    core_copy(0).wait_send()
+    core_copy(1).wait_send()
+    z_copy.wait_send()
+
+
+def exchange(strand_mean, w_rows, member):
+    rows, width = strand_mean.shape
+    cols = w_rows.shape[0]
+    vmem = pl.BlockSpec(memory_space=pltpu.VMEM)
+    total, group = 4 * rows, 4 * cols
+    return pl.pallas_call(
+        exchange_kernel,
+        out_shape=jax.ShapeDtypeStruct((4 * SUB, LANES), jnp.float32),
+        in_specs=[vmem] * 3,
+        out_specs=vmem,
+        scratch_shapes=[
+            pltpu.VMEM((total, width), jnp.bfloat16),
+            pltpu.VMEM((16 * cols, width), jnp.bfloat16),
+            pltpu.VMEM((2, total, group), jnp.float32),
+            pltpu.VMEM((2, total, group), jnp.float32),
+            pltpu.VMEM((total, group), jnp.bfloat16),
+            pltpu.VMEM((total, group), jnp.bfloat16),
+            pltpu.VMEM((64 * SUB, LANES), jnp.float32),
+            pltpu.VMEM((64 * SUB, LANES), jnp.float32),
+            pltpu.SemaphoreType.DMA((16,)),
+            pltpu.SemaphoreType.DMA((16,)),
+            pltpu.SemaphoreType.DMA((12,)),
+            pltpu.SemaphoreType.DMA((12,)),
+            pltpu.SemaphoreType.DMA((3,)),
+            pltpu.SemaphoreType.DMA((3,)),
+            pltpu.SemaphoreType.DMA,
+            pltpu.SemaphoreType.DMA,
+        ],
+        compiler_params=pltpu.CompilerParams(
+            vmem_limit_bytes=48 << 20, collective_id=0, has_side_effects=True
+        ),
+    )(strand_mean, w_rows, member)
+
+
 def body(tokens, complement, seg_lengths, owner, embed, norm_gain, taps, w_out):
     row_count = tokens.shape[0]
     vocab_size, width = embed.shape
-    ctx_count = lax.axis_size("ctx")
     ch_count = lax.axis_size("ch")
     place = lax.axis_index("ctx")
     full_width = width * ch_count
@@ -142,14 +416,7 @@
     block_total = owner.shape[0]
     per_block = seg_count // block_total
     near = 4
-    far = ctx_count // near
-    near_groups = [[near * m + y for y in range(near)] for m in range(far)]
-    far_groups = [[near * m + y for m in range(far)] for y in range(near)]
     out_cols = w_out.shape[1]
-
-    w_rows = lax.all_gather(
-        w_out.T, "ctx", axis=0, tiled=True, axis_index_groups=far_groups
-    )
 
     power = lax.psum(jnp.sum(jnp.square(embed.astype(jnp.float32)), axis=1), "ch")
     inv = lax.rsqrt(power / full_width + norm_eps)[:, None]
@@ -173,15 +440,6 @@
     strand_mean = mix_strands(
         tok_ext, complement, starts, ends, embed, inv, norm_gain[None, :], taps
     )
-    rows = lax.all_gather(
-        strand_mean, "ctx", axis=0, tiled=True, axis_index_groups=near_groups
-    )
-    terms = lax.dot_general(
-        rows, w_rows, (((1,), (1,)), ((), ())), preferred_element_type=jnp.float32
-    )
-    col_share = lax.psum_scatter(terms, "ch", scatter_dimension=1, tiled=True)
-    active = jax.nn.softplus(col_share)
-
     slots = jnp.arange(seg_count, dtype=jnp.int32)
     block_ids = jnp.arange(block_total, dtype=jnp.int32)
     holder = jnp.sum(
@@ -192,20 +450,10 @@
     slot_start = jnp.sum(jnp.where(same_seg, seg_starts[None, :], 0), axis=1)
     slot_end = jnp.sum(jnp.where(same_seg, seg_ends[None, :], 0), axis=1)
     group_pos = (place // near) * (near * row_count) + jnp.arange(near * row_count, dtype=jnp.int32)
-    member = (
-        (slot_start[:, None] <= group_pos[None, :]) & (group_pos[None, :] < slot_end[:, None])
-    ).astype(jnp.float32)
-    partial_sums = jnp.dot(member, active, precision=lax.Precision.HIGHEST)
-    share = partial_sums.shape[1]
-    received = lax.all_to_all(
-        partial_sums.reshape(ctx_count, per_block, share),
-        "ctx",
-        split_axis=0,
-        concat_axis=0,
-        tiled=True,
-    )
-    sums = jnp.sum(received.reshape(far, near, per_block, share), axis=0)
-    sums = sums.reshape(near, per_block, far // ch_count, out_cols)
+    group_pos = group_pos.reshape(near, 1, row_count)
+    member = (slot_start[None, :, None] <= group_pos) & (group_pos < slot_end[None, :, None])
+    sums = exchange(strand_mean, w_out.T, member.astype(jnp.bfloat16))
+    sums = sums.reshape(near, per_block, near, out_cols)
     totals = sums.transpose(1, 2, 0, 3).reshape(per_block, width)
     own_lengths = lax.dynamic_slice_in_dim(slot_end - slot_start, place * per_block, per_block)
     return totals / own_lengths.astype(jnp.float32)[:, None]

time: 207 us -> 93 us (0.45)
  waiting for transfers between devices: 133 us -> 0.01 us
  Pallas kernels: 16.7 us -> 73.6 us
  between operations: 13.2 us -> 0.22 us
  starting transfers between devices: 17.7 us -> 6.08 us
  matrix products: 6.29 us -> 0 us
  local copies, waits for them, and re-layouts: 5.33 us -> 0.36 us
    all_gather x2 -> x0, waiting for transfers between devices: 91.1 us -> none  [the longest x1 62.8 us: body(): lax.all_gather(w_out.T, 'ctx', axis=0, tiled=True, axis_index_groups=far_...]
    pallas_call x0 -> x1, Pallas kernels: none -> 57.6 us  [exchange(): pl.pallas_call(exchange_kernel, out_shape=jax.ShapeDtypeStruct((4 * SUB,...]
    reduce_scatter x1 -> x0, waiting for transfers between devices: 28.5 us -> none  [body(): col_share = lax.psum_scatter(terms, 'ch', scatter_dimension=1, tiled=True)]
    all_to_all x1 -> x0, waiting for transfers between devices: 13 us -> none  [body(): lax.all_to_all(partial_sums.reshape(ctx_count, per_block, share), 'ctx',...]
    all_to_all x1 -> x0, starting transfers between devices: 11.7 us -> none  [body(): lax.all_to_all(partial_sums.reshape(ctx_count, per_block, share), 'ctx',...]
    dot_general x2 -> x0, matrix products: 6.29 us -> none  [the longest x1 4.5 us: body(): lax.dot_general(rows, w_rows, (((1,), (1,)), ((), ())), preferred_element...]
    unnamed x10 -> x14, local copies, waits for them, and re-layouts: 4.22 us -> 0.03 us
  transfers between devices with their start and end apart: 6 -> 2, of which waited for: 4 -> 0; matrix products, arithmetic and copies ran while one was open for 2% -> 4% of each run, Pallas kernels for 0% -> 0%
where the time goes in v1:
time: 93 us; the launch traced here: 92.8 us
  Pallas kernels  73.6 us (79%)
  blocking collectives  8.13 us (9%)
  starting transfers between devices  6.08 us (7%)
  other arithmetic  4.44 us (5%)
    pallas_call x1, Pallas kernels, exchange(): pl.pallas_call(exchange_kernel, out_shape=jax.ShapeDtypeStruct((4 * SUB,...  57.6 us
    pallas_call x1, Pallas kernels, mix_strands(): pl.pallas_call(mix_kernel, out_shape=jax.ShapeDtypeStruct((count, width),...  15.9 us
    psum x1, blocking collectives, body(): lax.psum(jnp.sum(jnp.square(embed.astype(jnp.float32)), axis=1), 'ch')  8.13 us
    ppermute x2, starting transfers between devices, passed_along(): return lax.ppermute(array, axis, pairs)  6.08 us
  transfers between devices with their start and end apart: 2, of which 0 were waited for; matrix products, arithmetic and copies ran while one was open for 4% of the time, Pallas kernels for 0%

profile of v1, /device:TPU:1, one launch (start us, length us, event | category | flops | bytes accessed | tf_op | source)
XLA Modules:
  0.0 92.8 jit_solution(4730581162362201819)
XLA Ops:
  0.0 0.0 copy-start.4
  0.0 0.0 copy-start.3
  0.0 0.0 copy-start.1
  0.0 1.4 %collective-permute-start.1 = (s32[128]{0:T(128)}, s32[128]{0:T(128)S(1)}, u32[]{:S(2)}, u32[]{:S(2)}) collective-permute-start(s32[128]{0:T(128)} %param.8), channel_id=1, source_target_pairs={{4,0},{8,4},{12,8},{16,12},{20,16},{24,20},{28,24},{32,28},{36,32}... | collective-permute-start | bytes 1544 | tf_op jit(solution)/shard_map/ppermute | solution.py:17
  1.5 4.7 %collective-permute-start = (s32[128]{0:T(128)}, s32[128]{0:T(128)S(1)}, u32[]{:S(2)}, u32[]{:S(2)}) collective-permute-start(s32[128]{0:T(128)} %param.8), channel_id=1, source_target_pairs={{0,4},{4,8},{8,12},{12,16},{16,20},{20,24},{24,28},{28,32},{32,36}... | collective-permute-start | bytes 1544 | tf_op jit(solution)/shard_map/ppermute | solution.py:17
  6.2 0.8 select_reduce_fusion.2
  6.9 0.7 sub.24
  7.6 1.5 %multiply_reduce_fusion = f32[512]{0:T(512)S(1)} fusion(bf16[512,1024]{1,0:T(8,128)(2,1)} %embed_ref.1), kind=kLoop, calls=%fused_computation | loop fusion | flops 1572352 | bytes 1050624 | tf_op jit(solution)/shard_map/reduce_sum | solution.py:421
  9.1 8.1 %psum.7 = f32[512]{0:T(512)S(1)} all-reduce(f32[512]{0:T(512)S(1)} %multiply_reduce_fusion), channel_id=1, replica_groups=mesh['ctx'=64,'ch'=4] {'ch'}, use_global_device_ids=true, to_apply=%region_4.5 | all-reduce | flops 512 | bytes 4096 | tf_op jit(solution)/shard_map/psum | solution.py:421
  17.3 0.1 select_reduce_fusion.5
  17.4 0.2 select_reduce_fusion.3
  17.6 0.2 select_reduce_fusion.1
  17.8 0.2 and_convert_fusion.member_ref
  18.0 0.1 dynamic-slice_convert_fusion
  18.1 0.1 copy.12.inv_ref
  18.2 0.0 collective-permute-done.1
  18.2 0.0 collective-permute-done
  18.3 0.0 copy-done.6
  18.3 0.0 copy-start.2
  18.3 15.9 %shard_map.82.s_ref = bf16[128,1024]{1,0:T(8,128)(2,1)S(1)} custom-call(s32[384]{0:T(512)S(1)} %pad_add_fusion.tok_ref, s32[512]{0:T(512)S(1)} %copy-done.4, s32[128]{0:T(128)S(1)} %get-tuple-element.10.start_ref, s32[128]{0:T(128)S(1)} %get-tuple-element.9.end_ref, bf16[512,1024]{1,0:T(8,128)(2,1)S(1)} %copy-done, f32[512,1]{1,0:T(8,128)S(1)} %copy.12.inv_ref, ...), custom_call_target="tpu_custom_call" | custom-call | flops 67108864 | bytes 4194304 | tf_op jit(solution)/shard_map/pallas_call | solution.py:116
  34.3 57.6 %shard_map.83 = f32[32,128]{1,0:T(8,128)S(1)} custom-call(bf16[128,1024]{1,0:T(8,128)(2,1)S(1)} %shard_map.82.s_ref, bf16[64,1024]{1,0:T(8,128)(2,1)S(1)} %bitcast.4, bf16[4,256,128]{2,1,0:T(8,128)(2,1)S(1)} %and_convert_fusion.member_ref), custom_call_target="tpu_custom_call" | custom-call | tf_op jit(solution)/shard_map/pallas_call | solution.py:380
  91.9 0.1 reshape.52
  92.0 0.1 reshape.53
  92.1 0.7 broadcast_divide_fusion
  (18 shorter events, 0.1 us)
Async XLA Ops:
  0.0 18.3 %copy-start.6 = (s32[128]{0:T(128)S(1)}, s32[128]{0:T(128)}, u32[]{:S(2)}) copy-start(s32[128]{0:T(128)} %param.8) | copy-start | bytes 1540
  0.0 18.3 %copy-start = (bf16[512,1024]{1,0:T(8,128)(2,1)S(1)}, bf16[512,1024]{1,0:T(8,128)(2,1)}, u32[]{:S(2)}) copy-start(bf16[512,1024]{1,0:T(8,128)(2,1)} %embed_ref.1) | copy-start | bytes 3145732
  0.0 17.3 %copy-start.5 = (s32[64]{0:T(128)S(1)}, s32[64]{0:T(128)}, u32[]{:S(2)}) copy-start(s32[64]{0:T(128)} %param.11) | copy-start | bytes 772
  0.0 18.3 %copy-start.4 = (s32[512]{0:T(512)S(1)}, s32[512]{0:T(512)}, u32[]{:S(2)}) copy-start(s32[512]{0:T(512)} %comp_ref.1) | copy-start | bytes 6148
  0.0 18.3 %copy-start.3 = (f32[1024]{0:T(1024)S(1)}, f32[1024]{0:T(1024)}, u32[]{:S(2)}) copy-start(f32[1024]{0:T(1024)} %param.13) | copy-start | bytes 12292
  0.0 18.3 %copy-start.1 = (f32[128,1024]{1,0:T(8,128)S(1)}, f32[128,1024]{1,0:T(8,128)}, u32[]{:S(2)}) copy-start(f32[128,1024]{1,0:T(8,128)} %taps_ref.1) | copy-start | bytes 1572868
  0.0 18.2 %collective-permute-start.1 = (s32[128]{0:T(128)}, s32[128]{0:T(128)S(1)}, u32[]{:S(2)}, u32[]{:S(2)}) collective-permute-start(s32[128]{0:T(128)} %param.8), channel_id=1, source_target_pairs={{4,0},{8,4},{12,8},{16,12},{20,16},{24,20},{28,24},{32,28},{36,32}... | collective-permute-start | bytes 1544 | tf_op jit(solution)/shard_map/ppermute | solution.py:17
  1.5 16.8 %collective-permute-start = (s32[128]{0:T(128)}, s32[128]{0:T(128)S(1)}, u32[]{:S(2)}, u32[]{:S(2)}) collective-permute-start(s32[128]{0:T(128)} %param.8), channel_id=1, source_target_pairs={{0,4},{4,8},{8,12},{12,16},{16,20},{20,24},{24,28},{28,32},{32,36}... | collective-permute-start | bytes 1544 | tf_op jit(solution)/shard_map/ppermute | solution.py:17
  18.3 15.9 %copy-start.2 = (bf16[1024,64]{0,1:T(8,128)(2,1)S(1)}, bf16[1024,64]{0,1:T(8,128)(2,1)}, u32[]{:S(2)}) copy-start(bf16[1024,64]{0,1:T(8,128)(2,1)} %param.15) | copy-start | bytes 393220

commit v2 on v1

v2 whole, which is shorter than its diff:
```python
import jax
import jax.numpy as jnp
from jax import lax
from jax.experimental import pallas as pl
from jax.experimental.pallas import tpu as pltpu
from jax.sharding import PartitionSpec as P

norm_eps = 1e-06
LANES = 128
SUB = 8
PAD = 8
SPAN = 128
TAPROWS = 152
BASE = 143
MESH = pl.DeviceIdType.MESH
f32 = jnp.float32
bf16 = jnp.bfloat16


def rows3(ref, k, n):
    return ref[pl.ds(pl.multiple_of(k * SUB, SUB), n * SUB), :].reshape(n, SUB, LANES)

def put3(ref, k, v):
    n = v.shape[0]
    ref[pl.ds(pl.multiple_of(k * SUB, SUB), n * SUB), :] = v.reshape(n * SUB, LANES)

def prep_taps(taps_ref, tv, dv, tr, dr):
    span = taps_ref.shape[0]
    edge = jnp.zeros((PAD * SUB, LANES), jnp.float32)
    tv[pl.ds(0, PAD * SUB), :] = edge
    for e in range(2):
        tv[pl.ds((PAD + span + 8 * e) * SUB, 8 * SUB), :] = edge
    for s in range(SUB):
        tv[pl.ds(PAD * SUB + s, span, stride=SUB), :] = taps_ref[:, s * LANES:(s + 1) * LANES]
    dv[pl.ds(0, PAD * SUB), :] = edge
    dv[pl.ds(PAD * SUB, (TAPROWS - PAD) * SUB), :] = (
        tv[pl.ds(0, (TAPROWS - PAD) * SUB), :] - tv[pl.ds(PAD * SUB, (TAPROWS - PAD) * SUB), :])
    def flip(k8, carry):
        for u in range(8):
            k = k8 * 8 + u
            put3(tr, TAPROWS - 1 - k, rows3(tv, k, 1))
            put3(dr, TAPROWS - 1 - k, rows3(dv, k, 1))
        return carry
    lax.fori_loop(0, TAPROWS // 8, flip, 0)

def conv_block(i, count, ext_f, ext_r, tv, dv, tr, dr, sv, ev, res):
    p0 = i * 16
    zero8 = jnp.zeros((8, SUB, LANES), jnp.float32)
    idx16 = lax.broadcasted_iota(jnp.int32, (16, SUB, LANES), 0)
    far_lags = SPAN // 16
    s0 = rows3(sv, p0, 1)
    e0 = rows3(ev, p0 + 15, 1)

    def fwd_far(j, acc):
        lag = j * 16
        q0 = p0 - lag
        rows = jnp.where(idx16 >= s0 - q0, rows3(ext_f, count + q0, 16), 0.0)
        x0, x1 = rows[:8], rows[8:]
        xs = x0 + x1
        a, b, c = acc
        for u in range(8):
            a = a + rows3(tv, PAD + lag - u, 8) * xs[u:u + 1]
            b = b + rows3(dv, PAD + lag - u, 8) * x1[u:u + 1]
            c = c + rows3(dv, PAD + 8 + lag - u, 8) * x0[u:u + 1]
        return a, b, c

    def rev_far(j, acc):
        lag = j * 16
        q0 = p0 + lag
        rows = jnp.where(idx16 < e0 - q0, rows3(ext_r, q0, 16), 0.0)
        x0, x1 = rows[:8], rows[8:]
        xs = x0 + x1
        a, b, c = acc
        for u in range(8):
            a = a + rows3(tr, BASE - lag - u, 8) * xs[u:u + 1]
            b = b + rows3(dr, BASE - lag - u, 8) * x0[u:u + 1]
            c = c + rows3(dr, BASE - 8 - lag - u, 8) * x1[u:u + 1]
        return a, b, c

    a, b, c = lax.fori_loop(1, far_lags + 1, fwd_far, (zero8,) * 3, unroll=2)
    far_f = (a + b, a - c)
    a, b, c = lax.fori_loop(1, far_lags + 1, rev_far, (zero8,) * 3, unroll=2)
    far_r = (a - c, a + b)
    xf = (rows3(ext_f, count + p0, 8), rows3(ext_f, count + p0 + 8, 8))
    xr = (rows3(ext_r, p0, 8), rows3(ext_r, p0 + 8, 8))
    idx8 = lax.broadcasted_iota(jnp.int32, (8, SUB, LANES), 0)
    mid = rows3(sv, p0 + 8, 1)
    m = jnp.where(idx8 >= mid - p0, xf[0], 0.0)
    mid_f = zero8
    for u in range(8):
        mid_f = mid_f + rows3(tv, PAD + 8 - u, 8) * m[u:u + 1]
    mid = rows3(ev, p0 + 7, 1)
    m = jnp.where(idx8 < mid - p0 - 8, xr[1], 0.0)
    mid_r = zero8
    for u in range(8):
        mid_r = mid_r + rows3(tr, BASE - 8 - u, 8) * m[u:u + 1]
    for h in range(2):
        pb = p0 + 8 * h
        start = rows3(sv, pb, 8)
        end = rows3(ev, pb, 8)
        mix_f = jnp.where(start < p0, far_f[h], 0.0)
        mix_r = jnp.where(end > p0 + 16, far_r[h], 0.0)
        if h == 1:
            mix_f = mix_f + jnp.where(start < pb, mid_f, 0.0)
        else:
            mix_r = mix_r + jnp.where(end > pb + 8, mid_r, 0.0)
        for u in range(8):
            mix_f = mix_f + jnp.where(start <= pb + u, rows3(tv, PAD - u, 8) * xf[h][u:u + 1], 0.0)
            mix_r = mix_r + jnp.where(end > pb + u, rows3(tr, BASE - u, 8) * xr[h][u:u + 1], 0.0)
        gated_f = (xf[h] * mix_f).astype(jnp.bfloat16).astype(jnp.float32)
        gated_r = (xr[h] * mix_r).astype(jnp.bfloat16).astype(jnp.float32)
        put3(res, pb, (gated_f + gated_r) * 0.5)


def score_kernel(tok_ref, comp_ref, lens_ref, owner_ref, embed_ref, gain_ref, taps_ref, w_ref,
                 out_ref, sbuf, wbuf, out1, in1, zout, zin, pbuf, rbuf, member, scale,
                 tk, pw, ext_f, ext_r, tv, dv, tr, dr, sv, ev, res,
                 w_send, w_recv, s_send, s_recv, r_send, r_recv, a_send, a_recv,
                 t_send, t_recv, p_send, p_recv):
    me = lax.axis_index("ctx")
    ch = lax.axis_index("ch")
    peers = lax.axis_size("ctx")
    y = lax.rem(me, 4)
    zh = lax.rem(lax.div(me, 4), 4)
    x = lax.div(me, 16)
    zl = lax.div(ch, 2)
    core = lax.rem(ch, 2)

    def ring(v, by):
        return lax.rem(v + by, 4)

    xp, xm, x2 = ring(x, 1), ring(x, 3), ring(x, 2)
    zp, zm, z2 = ring(zh, 1), ring(zh, 3), ring(zh, 2)
    yp, ym, y2 = ring(y, 1), ring(y, 3), ring(y, 2)
    core_peer = zl * 2 + 1 - core
    z_peer = (1 - zl) * 2 + core

    barrier = pltpu.get_barrier_semaphore()

    def hello(d, carry):
        pl.semaphore_signal(
            barrier, inc=1, device_id={"ctx": lax.rem(me + d, peers)}, device_id_type=MESH
        )
        return carry

    lax.fori_loop(1, peers, hello, 0)
    for d in range(1, 4):
        pl.semaphore_signal(
            barrier, inc=1, device_id={"ch": lax.rem(ch + d, 4)}, device_id_type=MESH
        )

    cols = w_ref.shape[0]
    half = cols // 2
    rows = sbuf.shape[0] // 4
    vocab, width = embed_ref.shape
    segs = lens_ref.shape[1]

    fold = jnp.zeros((vocab, LANES), f32)
    for s in range(SUB):
        piece = embed_ref[:, s * LANES : (s + 1) * LANES].astype(f32)
        fold = fold + piece * piece
    pw[ch] = jnp.broadcast_to(jnp.sum(fold.T, axis=0, keepdims=True), (SUB, vocab))
    tk[1] = jnp.broadcast_to(tok_ref[...], (SUB, rows))

    def iota(shape, dim):
        return lax.broadcasted_iota(jnp.int32, shape, dim)

    lens = jnp.broadcast_to(lens_ref[...], (SUB, segs)).astype(f32)
    upto = (iota((segs, segs), 0) <= iota((segs, segs), 1)).astype(bf16)
    ends_row = jnp.dot(lens.astype(bf16), upto, preferred_element_type=f32)
    starts_row = (ends_row - lens)[0:1]
    ends_row = ends_row[0:1]
    first = me * rows
    pos = (iota((rows, segs), 0) + first).astype(f32)
    start_col = jnp.max(jnp.where(starts_row <= pos, starts_row, 0.0), axis=1, keepdims=True)
    end_col = jnp.min(jnp.where(ends_row > pos, ends_row, 1e9), axis=1, keepdims=True)
    start_col = jnp.broadcast_to(start_col, (rows, LANES)).astype(jnp.int32) - first
    end_col = jnp.broadcast_to(end_col, (rows, LANES)).astype(jnp.int32) - first
    for s in range(SUB):
        sv[pl.ds(s, rows, stride=SUB), :] = start_col
        ev[pl.ds(s, rows, stride=SUB), :] = end_col

    blocks = owner_ref.shape[1]
    spread = ((iota((blocks, segs), 1) >> 2) == iota((blocks, segs), 0)).astype(bf16)
    owners = jnp.broadcast_to(owner_ref[...], (SUB, blocks)).astype(f32).astype(bf16)
    owner_row = jnp.dot(owners, spread, preferred_element_type=f32)[0:1].astype(jnp.int32)
    slot, seg = iota((segs, segs), 0), iota((segs, segs), 1)
    same = (owner_row == (slot >> 2)) & ((slot & 3) == (seg & 3))
    slot_start = jnp.sum(jnp.where(same, starts_row, 0.0), axis=1, keepdims=True)
    slot_end = jnp.sum(jnp.where(same, ends_row, 0.0), axis=1, keepdims=True)
    total = 4 * rows
    spot = (iota((segs, total), 1) + lax.div(me, 4) * total).astype(f32)
    member[...] = ((slot_start <= spot) & (spot < slot_end)).astype(f32).astype(bf16)
    scale[...] = jnp.broadcast_to(slot_end - slot_start, (segs, LANES))

    prep_taps(taps_ref, tv, dv, tr, dr)
    pl.semaphore_wait(barrier, peers + 2)
    parts = 4
    chunk = rows // parts

    def at_ctx(cx, cz, cy):
        return {"ctx": cx * 16 + cz * 4 + cy}

    def w_rows(cx, cz, lo=0, count=cols):
        return wbuf.at[pl.ds(pl.multiple_of((cx * 4 + cz) * cols + lo, half), count), :]

    def w_copy(label, src, dst, to):
        return pltpu.make_async_remote_copy(
            src_ref=src, dst_ref=dst, send_sem=w_send.at[label], recv_sem=w_recv.at[label],
            device_id=to, device_id_type=MESH,
        )

    z_of = (zh, zm, zp, z2)
    plus, minus = at_ctx(xp, zh, y), at_ctx(xm, zh, y)
    up, down = at_ctx(x, zp, y), at_ctx(x, zm, y)
    own = w_rows(x, zh)
    sent = {
        0: (w_ref, own, up),
        1: (w_ref, own, down),
        2: (w_rows(x, zm, 0, half), w_rows(x, zm, 0, half), up),
        3: (w_rows(x, zp, half, half), w_rows(x, zp, half, half), down),
    }
    got = {
        0: w_rows(x, zm),
        1: w_rows(x, zp),
        2: w_rows(x, z2, 0, half),
        3: w_rows(x, z2, half, half),
    }
    for dz in range(4):
        base = 4 + 3 * dz
        here = w_rows(x, z_of[dz])
        src = w_ref if dz == 0 else here
        sent[base] = (src, here, plus)
        sent[base + 1] = (src, here, minus)
        relay = w_rows(xm if dz < 2 else xp, z_of[dz])
        sent[base + 2] = (relay, relay, plus if dz < 2 else minus)
        got[base] = w_rows(xm, z_of[dz])
        got[base + 1] = w_rows(xp, z_of[dz])
        got[base + 2] = w_rows(x2, z_of[dz])

    def w_start(*labels):
        for n in labels:
            w_copy(n, *sent[n]).start()

    def w_wait(*labels):
        for n in labels:
            w_copy(n, got[n], got[n], plus).wait_recv()

    def s_rows(cy, k):
        return sbuf.at[pl.ds(pl.multiple_of(cy * rows + k * chunk, chunk), chunk), :]

    s_plus, s_minus = at_ctx(x, zh, yp), at_ctx(x, zh, ym)

    def s_copy(k, kind, src, dst, to):
        return pltpu.make_async_remote_copy(
            src_ref=src, dst_ref=dst, send_sem=s_send.at[3 * k + kind],
            recv_sem=s_recv.at[3 * k + kind], device_id=to, device_id_type=MESH,
        )

    def s_sent(k, kind):
        if kind < 2:
            return s_copy(
                k, kind, s_rows(y, k), s_rows(y, k),
                s_plus if kind == 0 else s_minus,
            )
        relay = s_rows(ym if k % 2 == 0 else yp, k)
        return s_copy(k, kind, relay, relay, s_plus if k % 2 == 0 else s_minus)

    def s_wait(k, kind):
        there = s_rows((ym, yp, y2)[kind], k)
        s_copy(k, kind, there, there, s_plus).wait_recv()

    def token_copy(slot, to):
        return pltpu.make_async_remote_copy(
            src_ref=tk.at[1], dst_ref=tk.at[slot], send_sem=t_send.at[slot // 2],
            recv_sem=t_recv.at[slot // 2], device_id={"ctx": to}, device_id_type=MESH,
        )

    def power_copy(d):
        return pltpu.make_async_remote_copy(
            src_ref=pw.at[ch], dst_ref=pw.at[ch], send_sem=p_send.at[d - 1],
            recv_sem=p_recv.at[d - 1], device_id={"ch": lax.rem(ch + d, 4)}, device_id_type=MESH,
        )

    def power_got(d):
        there = pw.at[lax.rem(ch + 4 - d, 4)]
        return pltpu.make_async_remote_copy(
            src_ref=there, dst_ref=there, send_sem=p_send.at[d - 1],
            recv_sem=p_recv.at[d - 1], device_id={"ch": lax.rem(ch + d, 4)}, device_id_type=MESH,
        )

    after, before = lax.rem(me + 1, peers), lax.rem(me + peers - 1, peers)
    for d in range(1, 4):
        power_copy(d).start()
    token_copy(0, after).start()
    token_copy(2, before).start()
    w_start(0, 1, 4, 5)
    wbuf[pl.ds(pl.multiple_of((x * 4 + zh) * cols, cols), cols), :] = w_ref[...]

    token_copy(0, after).wait_recv()
    token_copy(2, before).wait_recv()
    for d in range(1, 4):
        power_got(d).wait_recv()
    power = (pw[0] + pw[1]) + (pw[2] + pw[3])
    inv = lax.rsqrt(power / (4 * width) + norm_eps).T[:, 0:1]
    letters = iota((rows, vocab), 1)
    picks_f, picks_r = [], []
    for q in range(3):
        ids = tk[q].astype(f32).T[:, 0:1].astype(jnp.int32)
        hit = letters == ids
        if q < 2:
            picks_f.append(hit.astype(f32).astype(bf16))
        if q > 0:
            other = jnp.sum(
                jnp.where(hit, comp_ref[...].astype(f32), 0.0), axis=1, keepdims=True
            ).astype(jnp.int32)
            picks_r.append((letters == other).astype(f32).astype(bf16))
    for s in range(SUB):
        lanes = slice(s * LANES, (s + 1) * LANES)
        table = (embed_ref[:, lanes].astype(f32) * inv * gain_ref[:, lanes]).astype(bf16)
        for q in range(2):
            at = pl.ds(q * rows * SUB + s, rows, stride=SUB)
            ext_f[at, :] = jnp.dot(picks_f[q], table, preferred_element_type=f32)
            ext_r[at, :] = jnp.dot(picks_r[q], table, preferred_element_type=f32)

    w_wait(0)
    w_start(2, 7, 8)
    w_wait(1)
    w_start(3, 10, 11)
    w_wait(4)
    w_start(6)
    for k in range(parts):
        def two(i, carry, k=k):
            conv_block(2 * k + i, rows, ext_f, ext_r, tv, dv, tr, dr, sv, ev, res)
            return carry

        lax.fori_loop(0, chunk // 16, two, 0)
        at = pl.ds(pl.multiple_of(y * rows + k * chunk, chunk), chunk)
        for s in range(SUB):
            got_rows = res[pl.ds(k * chunk * SUB + s, chunk, stride=SUB), :]
            sbuf[at, s * LANES : (s + 1) * LANES] = got_rows.astype(bf16)
        s_sent(k, 0).start()
        s_sent(k, 1).start()
        if k == 0:
            w_wait(2, 3)
            w_start(13, 14)
        elif k == 1:
            w_wait(7)
            w_start(9)
        elif k == 2:
            w_wait(11)
            w_start(12)
        else:
            w_wait(14)
            w_start(15)
        if k > 0:
            s_wait(k - 1, (k - 1) % 2)
            s_sent(k - 1, 2).start()
    s_wait(parts - 1, (parts - 1) % 2)
    s_sent(parts - 1, 2).start()
    for k in range(parts):
        s_wait(k, 1 - k % 2)
        s_wait(k, 2)
    w_wait(5, 6, 8, 9, 10, 12, 13, 15)

    group = 4 * cols

    def product(g):
        rhs = wbuf[pl.ds(pl.multiple_of(g * group, group), group), :]
        return lax.dot_general(
            sbuf[...], rhs, (((1,), (1,)), ((), ())), preferred_element_type=f32
        )

    def core_copy(slot):
        return pltpu.make_async_remote_copy(
            src_ref=out1.at[slot], dst_ref=in1.at[slot], send_sem=r_send.at[slot],
            recv_sem=r_recv.at[slot], device_id={"ch": core_peer}, device_id_type=MESH,
        )

    z_copy = pltpu.make_async_remote_copy(
        src_ref=zout, dst_ref=zin, send_sem=r_send.at[2], recv_sem=r_recv.at[2],
        device_id={"ch": z_peer}, device_id_type=MESH,
    )
    out1[0] = product(2 * (1 - zl) + 1 - core)
    core_copy(0).start()
    out1[1] = product(2 * zl + 1 - core)
    core_copy(1).start()
    own_part = product(2 * (1 - zl) + core)
    core_copy(0).wait_recv()
    zout[...] = (own_part + in1[0]).astype(bf16)
    z_copy.start()
    own_part = product(2 * zl + core)
    core_copy(1).wait_recv()
    in1[1] = own_part + in1[1]
    z_copy.wait_recv()

    def sum_up(t, acc):
        at = pl.ds(pl.multiple_of(t * rows, rows), rows)
        scores = in1[1, at, :] + zin[at, :].astype(f32)
        active = jnp.maximum(scores, 0.0) + jnp.log1p(jnp.exp(-jnp.abs(scores)))
        high = active.astype(bf16)
        low = (active - high.astype(f32)).astype(bf16)
        picks = member[:, pl.ds(pl.multiple_of(t * rows, rows), rows)]
        return (
            acc
            + jnp.dot(picks, high, preferred_element_type=f32)
            + jnp.dot(picks, low, preferred_element_type=f32)
        )

    sums = lax.fori_loop(0, 4, sum_up, jnp.zeros((segs, group), f32))
    wide = group // LANES
    for h in range(wide):
        pbuf[pl.ds(h, segs, stride=wide), :] = sums[:, h * LANES : (h + 1) * LANES] / scale[...]

    def to_owner(d, carry):
        dest = lax.rem(me + d, peers)
        pltpu.make_async_remote_copy(
            src_ref=pbuf.at[pl.ds(pl.multiple_of(dest * SUB, SUB), SUB), :],
            dst_ref=rbuf.at[pl.ds(pl.multiple_of(me * SUB, SUB), SUB), :],
            send_sem=a_send, recv_sem=a_recv, device_id={"ctx": dest}, device_id_type=MESH,
        ).start()
        return carry

    lax.fori_loop(1, peers, to_owner, 0)
    mine = pl.ds(pl.multiple_of(me * SUB, SUB), SUB)
    rbuf[mine, :] = pbuf[mine, :]
    most = pl.ds(0, (peers - 1) * SUB)
    all_of = pltpu.make_async_remote_copy(
        src_ref=pbuf.at[most, :], dst_ref=rbuf.at[most, :], send_sem=a_send, recv_sem=a_recv,
        device_id={"ctx": lax.rem(me + 1, peers)}, device_id_type=MESH,
    )
    all_of.wait_recv()
    for q in range(4):
        acc = rbuf[pl.ds(q * SUB, SUB), :]
        for m in range(1, peers // 4):
            acc = acc + rbuf[pl.ds((4 * m + q) * SUB, SUB), :]
        out_ref[pl.ds(q * SUB, SUB), :] = acc
    all_of.wait_send()
    for n in range(16):
        w_copy(n, *sent[n]).wait_send()
    for k in range(parts):
        for kind in range(3):
            s_sent(k, kind).wait_send()
    for d in range(1, 4):
        power_copy(d).wait_send()
    token_copy(0, after).wait_send()
    token_copy(2, before).wait_send()
    core_copy(0).wait_send()
    core_copy(1).wait_send()
    z_copy.wait_send()


def body(tokens, complement, seg_lengths, owner, embed, norm_gain, taps, w_out):
    rows = tokens.shape[0]
    vocab, width = embed.shape
    cols = w_out.shape[1]
    segs = seg_lengths.shape[0]
    per_block = segs // owner.shape[0]
    total, group = 4 * rows, 4 * cols
    peers = owner.shape[0]
    vmem = pl.BlockSpec(memory_space=pltpu.VMEM)

    def tiles(count, dtype=f32):
        return pltpu.VMEM((count * SUB, LANES), dtype)

    def sems(count):
        return pltpu.SemaphoreType.DMA((count,))

    sums = pl.pallas_call(
        score_kernel,
        out_shape=jax.ShapeDtypeStruct((4 * SUB, LANES), f32),
        in_specs=[vmem] * 8,
        out_specs=vmem,
        scratch_shapes=[
            pltpu.VMEM((total, width), bf16),
            pltpu.VMEM((16 * cols, width), bf16),
            pltpu.VMEM((2, total, group), f32),
            pltpu.VMEM((2, total, group), f32),
            pltpu.VMEM((total, group), bf16),
            pltpu.VMEM((total, group), bf16),
            tiles(peers),
            tiles(peers),
            pltpu.VMEM((segs, total), bf16),
            pltpu.VMEM((segs, LANES), f32),
            pltpu.VMEM((3, SUB, rows), jnp.int32),
            pltpu.VMEM((4, SUB, vocab), f32),
            tiles(2 * rows),
            tiles(2 * rows),
            tiles(TAPROWS),
            tiles(TAPROWS),
            tiles(TAPROWS),
            tiles(TAPROWS),
            tiles(rows, jnp.int32),
            tiles(rows, jnp.int32),
            tiles(rows),
            sems(16),
            sems(16),
            sems(12),
            sems(12),
            sems(3),
            sems(3),
            pltpu.SemaphoreType.DMA,
            pltpu.SemaphoreType.DMA,
            sems(2),
            sems(2),
            sems(3),
            sems(3),
        ],
        compiler_params=pltpu.CompilerParams(
            vmem_limit_bytes=56 << 20, collective_id=0, has_side_effects=True
        ),
    )(
        tokens[None, :], complement[None, :], seg_lengths[None, :], owner[None, :],
        embed, norm_gain[None, :], taps, w_out.T,
    )
    sums = sums.reshape(4, per_block, 4, cols)
    return sums.transpose(1, 2, 0, 3).reshape(per_block, width)


def solution(mesh):
    in_specs = (P("ctx"), P(), P(), P(), P(None, "ch"), P("ch"), P(None, "ch"), P("ch", "ctx"))
    out_specs = P("ctx", "ch")
    return jax.shard_map(body, mesh=mesh, in_specs=in_specs, out_specs=out_specs, check_vma=False)
```

time: 93 us -> 67.2 us (0.72)
  Pallas kernels: 73.6 us -> 65.4 us
  blocking collectives: 8.13 us -> 0 us
  starting transfers between devices: 6.08 us -> 0 us
  other arithmetic: 4.44 us -> 0 us
  local copies, waits for them, and re-layouts: 0.36 us -> 1.51 us
    psum x1 -> x0, blocking collectives: 8.13 us -> none  [body(): lax.psum(jnp.sum(jnp.square(embed.astype(jnp.float32)), axis=1), 'ch')]
    pallas_call x2 -> x1, Pallas kernels: 73.6 us -> 65.4 us  [body(): pl.pallas_call(score_kernel, out_shape=jax.ShapeDtypeStruct((4 * SUB, LAN...]
    ppermute x2 -> x0, starting transfers between devices: 6.08 us -> none  [passed_along(): return lax.ppermute(array, axis, pairs)]
    reduce_sum x5 -> x0, other arithmetic: 2.79 us -> none  [the longest x1 1.5 us: body(): jnp.sum(jnp.square(embed.astype(jnp.float32)), axis=1)]
    reshape x2, local copies, waits for them, and re-layouts: 0.17 us -> 1.49 us  [the longest x1 0.8 us: body(): sums = sums.reshape(4, per_block, 4, cols)]
  transfers between devices with their start and end apart: 2 -> 0, of which waited for: 0 -> 0; matrix products, arithmetic and copies ran while one was open for 4% -> 0% of each run, Pallas kernels for 0% -> 0%
where the time goes in v2:
time: 67.2 us; the launch traced here: 67 us
  Pallas kernels  65.4 us (97%)
  local copies, waits for them, and re-layouts  1.51 us (2%)
    pallas_call x1, Pallas kernels, body(): pl.pallas_call(score_kernel, out_shape=jax.ShapeDtypeStruct((4 * SUB, LAN...  65.4 us

profile of v2, /device:TPU:1, one launch (start us, length us, event | category | flops | bytes accessed | tf_op | source)
XLA Modules:
  0.0 67.0 jit_solution(1244468020347464324)
XLA Ops:
  0.0 65.4 %shard_map.82 = f32[32,128]{1,0:T(8,128)} custom-call(s32[1,128]{1,0:T(1,128)} %bitcast.12, s32[1,512]{1,0:T(1,128)} %bitcast.10, s32[1,256]{1,0:T(1,128)} %bitcast.11, s32[1,64]{1,0:T(1,128)} %bitcast.13, bf16[512,1024]{1,0:T(8,128)(2,1)} %embed_ref.1, f32[1,1024]{1,0:T(1,128)} %bitcast.9, f32[128,1024]{1,0:T(8,128)} %taps_ref.1, bf16[64,1024]{1,0:T(8,128)(2,1)} %bitcast.8), custom_call_target="tpu_custom_call" | custom-call | tf_op jit(solution)/shard_map/pallas_call | solution.py:469
  65.5 0.8 %reshape.6 = f32[4,4,4,64]{3,2,1,0:T(4,128)S(1)} reshape(f32[32,128]{1,0:T(8,128)} %shard_map.82) | data formatting | bytes 32768 | tf_op jit(solution)/shard_map/reshape | solution.py:516
  66.3 0.7 %reshape.7 = f32[4,1024]{1,0:T(4,128)} reshape(f32[4,4,4,64]{3,2,1,0:T(4,128)S(1)} %copy.9) | data formatting | bytes 32768 | tf_op jit(solution)/shard_map/reshape | solution.py:517
  (1 shorter events, 0.0 us)

commit v3 on v2

v3 whole, which is shorter than its diff:
```python
import jax
import jax.numpy as jnp
from jax import lax
from jax.experimental import pallas as pl
from jax.experimental.pallas import tpu as pltpu
from jax.sharding import PartitionSpec as P

norm_eps = 1e-06
LANES = 128
SUB = 8
PAD = 8
SPAN = 128
TAPROWS = 152
BASE = 143
MESH = pl.DeviceIdType.MESH
f32 = jnp.float32
bf16 = jnp.bfloat16


def rows3(ref, k, n):
    return ref[pl.ds(pl.multiple_of(k * SUB, SUB), n * SUB), :].reshape(n, SUB, LANES)

def put3(ref, k, v):
    n = v.shape[0]
    ref[pl.ds(pl.multiple_of(k * SUB, SUB), n * SUB), :] = v.reshape(n * SUB, LANES)

def prep_taps(taps_ref, tv, dv, tr, dr):
    span = taps_ref.shape[0]
    edge = jnp.zeros((PAD * SUB, LANES), jnp.float32)
    tv[pl.ds(0, PAD * SUB), :] = edge
    for e in range(2):
        tv[pl.ds((PAD + span + 8 * e) * SUB, 8 * SUB), :] = edge
    for s in range(SUB):
        tv[pl.ds(PAD * SUB + s, span, stride=SUB), :] = taps_ref[:, s * LANES:(s + 1) * LANES]
    dv[pl.ds(0, PAD * SUB), :] = edge
    dv[pl.ds(PAD * SUB, (TAPROWS - PAD) * SUB), :] = (
        tv[pl.ds(0, (TAPROWS - PAD) * SUB), :] - tv[pl.ds(PAD * SUB, (TAPROWS - PAD) * SUB), :])
    def flip(k8, carry):
        for u in range(8):
            k = k8 * 8 + u
            put3(tr, TAPROWS - 1 - k, rows3(tv, k, 1))
            put3(dr, TAPROWS - 1 - k, rows3(dv, k, 1))
        return carry
    lax.fori_loop(0, TAPROWS // 8, flip, 0)

def conv_block(i, count, ext_f, ext_r, tv, dv, tr, dr, sv, ev, res):
    p0 = i * 16
    zero8 = jnp.zeros((8, SUB, LANES), jnp.float32)
    idx16 = lax.broadcasted_iota(jnp.int32, (16, SUB, LANES), 0)
    far_lags = SPAN // 16
    s0 = rows3(sv, p0, 1)
    e0 = rows3(ev, p0 + 15, 1)

    def fwd_far(j, acc):
        lag = j * 16
        q0 = p0 - lag
        rows = jnp.where(idx16 >= s0 - q0, rows3(ext_f, count + q0, 16), 0.0)
        x0, x1 = rows[:8], rows[8:]
        xs = x0 + x1
        a, b, c = acc
        for u in range(8):
            a = a + rows3(tv, PAD + lag - u, 8) * xs[u:u + 1]
            b = b + rows3(dv, PAD + lag - u, 8) * x1[u:u + 1]
            c = c + rows3(dv, PAD + 8 + lag - u, 8) * x0[u:u + 1]
        return a, b, c

    def rev_far(j, acc):
        lag = j * 16
        q0 = p0 + lag
        rows = jnp.where(idx16 < e0 - q0, rows3(ext_r, q0, 16), 0.0)
        x0, x1 = rows[:8], rows[8:]
        xs = x0 + x1
        a, b, c = acc
        for u in range(8):
            a = a + rows3(tr, BASE - lag - u, 8) * xs[u:u + 1]
            b = b + rows3(dr, BASE - lag - u, 8) * x0[u:u + 1]
            c = c + rows3(dr, BASE - 8 - lag - u, 8) * x1[u:u + 1]
        return a, b, c

    a, b, c = lax.fori_loop(1, far_lags + 1, fwd_far, (zero8,) * 3, unroll=2)
    far_f = (a + b, a - c)
    a, b, c = lax.fori_loop(1, far_lags + 1, rev_far, (zero8,) * 3, unroll=2)
    far_r = (a - c, a + b)
    xf = (rows3(ext_f, count + p0, 8), rows3(ext_f, count + p0 + 8, 8))
    xr = (rows3(ext_r, p0, 8), rows3(ext_r, p0 + 8, 8))
    idx8 = lax.broadcasted_iota(jnp.int32, (8, SUB, LANES), 0)
    mid = rows3(sv, p0 + 8, 1)
    m = jnp.where(idx8 >= mid - p0, xf[0], 0.0)
    mid_f = zero8
    for u in range(8):
        mid_f = mid_f + rows3(tv, PAD + 8 - u, 8) * m[u:u + 1]
    mid = rows3(ev, p0 + 7, 1)
    m = jnp.where(idx8 < mid - p0 - 8, xr[1], 0.0)
    mid_r = zero8
    for u in range(8):
        mid_r = mid_r + rows3(tr, BASE - 8 - u, 8) * m[u:u + 1]
    for h in range(2):
        pb = p0 + 8 * h
        start = rows3(sv, pb, 8)
        end = rows3(ev, pb, 8)
        mix_f = jnp.where(start < p0, far_f[h], 0.0)
        mix_r = jnp.where(end > p0 + 16, far_r[h], 0.0)
        if h == 1:
            mix_f = mix_f + jnp.where(start < pb, mid_f, 0.0)
        else:
            mix_r = mix_r + jnp.where(end > pb + 8, mid_r, 0.0)
        near_f = [rows3(tv, PAD + d, 1) for d in range(8)]
        sums_f, sums_r = [], []
        for r in range(8):
            sum_f, sum_r = mix_f[r : r + 1], mix_r[r : r + 1]
            for u in range(8):
                if u < r:
                    term = near_f[r - u] * xf[h][u : u + 1]
                    sum_f = sum_f + jnp.where(start[r : r + 1] <= pb + u, term, 0.0)
                elif u > r:
                    term = near_f[u - r] * xr[h][u : u + 1]
                    sum_r = sum_r + jnp.where(end[r : r + 1] > pb + u, term, 0.0)
            sums_f.append(sum_f + near_f[0] * xf[h][r : r + 1])
            sums_r.append(sum_r + near_f[0] * xr[h][r : r + 1])
        mix_f = jnp.concatenate(sums_f, axis=0)
        mix_r = jnp.concatenate(sums_r, axis=0)
        gated_f = (xf[h] * mix_f).astype(jnp.bfloat16).astype(jnp.float32)
        gated_r = (xr[h] * mix_r).astype(jnp.bfloat16).astype(jnp.float32)
        put3(res, pb, (gated_f + gated_r) * 0.5)


def score_kernel(tok_ref, comp_ref, lens_ref, owner_ref, gain_ref, embed_hbm, taps_hbm, w_hbm,
                 out_ref, embed_ref, taps_ref, sbuf, wbuf, out1, in1, zout, zin, kept,
                 pbuf, xbuf, abuf, rbuf, obuf, member, scale, tk, pw, gain8,
                 ext_f, ext_r, inv_f, inv_r, tv, dv, tr, dr, sv, ev, res,
                 l_sem, w_send, w_recv, s_send, s_recv, r_send, r_recv, z_send, z_recv,
                 x_send, x_recv, a_send, a_recv, t_send, t_recv, p_send, p_recv):
    me = lax.axis_index("ctx")
    ch = lax.axis_index("ch")
    peers = lax.axis_size("ctx")
    y = lax.rem(me, 4)
    zh = lax.rem(lax.div(me, 4), 4)
    x = lax.div(me, 16)
    zl = lax.div(ch, 2)
    core = lax.rem(ch, 2)

    def ring(v, by):
        return lax.rem(v + by, 4)

    def at_ctx(cx, cz, cy):
        return {"ctx": cx * 16 + cz * 4 + cy}

    xp, xm, x2 = ring(x, 1), ring(x, 3), ring(x, 2)
    zp, zm, z2 = ring(zh, 1), ring(zh, 3), ring(zh, 2)
    yp, ym, y2 = ring(y, 1), ring(y, 3), ring(y, 2)
    core_peer = zl * 2 + 1 - core
    z_peer = (1 - zl) * 2 + core
    after, before = lax.rem(me + 1, peers), lax.rem(me + peers - 1, peers)

    barrier = pltpu.get_barrier_semaphore()

    def greet(to):
        pl.semaphore_signal(barrier, inc=1, device_id=to, device_id_type=MESH)

    for d in range(1, 4):
        greet({"ch": lax.rem(ch + d, 4)})
        greet(at_ctx(ring(x, d), zh, y))
    greet({"ctx": after})
    greet({"ctx": before})

    def plane(d):
        return at_ctx(x, ring(zh, lax.div(d, 4)), ring(y, lax.rem(d, 4)))

    def hello(d, carry):
        greet(plane(d))
        return carry

    lax.fori_loop(1, 16, hello, 0)

    cols = w_hbm.shape[0]
    half = cols // 2
    rows = sbuf.shape[0] // 4
    vocab, width = embed_ref.shape
    segs = lens_ref.shape[1]
    own_w = wbuf.at[pl.ds(pl.multiple_of((x * 4 + zh) * cols, cols), cols), :]
    fetch = [
        pltpu.make_async_copy(embed_hbm, embed_ref, l_sem.at[0]),
        pltpu.make_async_copy(w_hbm, own_w, l_sem.at[1]),
        pltpu.make_async_copy(taps_hbm, taps_ref, l_sem.at[2]),
    ]
    for copy in fetch:
        copy.start()

    def iota(shape, dim):
        return lax.broadcasted_iota(jnp.int32, shape, dim)

    lens = jnp.broadcast_to(lens_ref[...], (SUB, segs)).astype(f32)
    upto = (iota((segs, segs), 0) <= iota((segs, segs), 1)).astype(bf16)
    ends_row = jnp.dot(lens.astype(bf16), upto, preferred_element_type=f32)
    starts_row = (ends_row - lens)[0:1]
    ends_row = ends_row[0:1]
    letters = iota((rows, vocab), 1)

    def ids_of(slot):
        return tk[slot].astype(f32).T[:, 0:1].astype(jnp.int32)

    def other_of(ids):
        hit = jnp.where(letters == ids, comp_ref[...].astype(f32), 0.0)
        return jnp.sum(hit, axis=1, keepdims=True).astype(jnp.int32)

    def pick_rows(ids_a, ids_b, put_a, put_b):
        picks = jnp.concatenate([letters == ids_a, letters == ids_b], axis=0)
        picks = picks.astype(f32).astype(bf16)
        for n in range(width // (2 * LANES)):
            table = embed_ref[:, n * 2 * LANES : (n + 1) * 2 * LANES]
            found = jnp.dot(picks, table, preferred_element_type=f32)
            for m in range(2):
                lanes = slice(m * LANES, (m + 1) * LANES)
                for ref, at, part in (put_a + (found[:rows],), put_b + (found[rows:],)):
                    ref[pl.ds(at * SUB + 2 * n + m, rows, stride=SUB), :] = part[:, lanes]

    tk[1] = jnp.broadcast_to(tok_ref[...], (SUB, rows))
    own_ids = ids_of(1)
    own_other = other_of(own_ids)

    fetch[0].wait()
    fold = jnp.zeros((vocab, LANES), f32)
    for s in range(SUB):
        piece = embed_ref[:, s * LANES : (s + 1) * LANES].astype(f32)
        fold = fold + piece * piece
        gain8[s : s + 1, :] = gain_ref[:, s * LANES : (s + 1) * LANES]
    pw[ch] = jnp.broadcast_to(jnp.sum(fold.T, axis=0, keepdims=True), (SUB, vocab))
    fetch[1].wait()

    def w_rows(cx, cz, h=None):
        lo, count = (0, cols) if h is None else (h * half, half)
        return wbuf.at[pl.ds(pl.multiple_of((cx * 4 + cz) * cols + lo, half), count), :]

    z_of = (zh, zm, zp, z2)
    plus, minus = at_ctx(xp, zh, y), at_ctx(xm, zh, y)
    up, down = at_ctx(x, zp, y), at_ctx(x, zm, y)
    sent, got = {}, {}
    for h in range(2):
        own = w_rows(x, zh, h)
        sent["z", h, 0], got["z", h, 0] = (own, up), w_rows(x, zm, h)
        sent["z", h, 1], got["z", h, 1] = (own, down), w_rows(x, zp, h)
        for dz in range(4):
            here = w_rows(x, z_of[dz], h)
            sent["x", dz, h, 0], got["x", dz, h, 0] = (here, plus), w_rows(xm, z_of[dz], h)
            sent["x", dz, h, 1], got["x", dz, h, 1] = (here, minus), w_rows(xp, z_of[dz], h)
    sent["y", 0], got["y", 0] = (w_rows(x, zm, 0), up), w_rows(x, z2, 0)
    sent["y", 1], got["y", 1] = (w_rows(x, zp, 1), down), w_rows(x, z2, 1)
    for dz in range(4):
        sent["r", dz, 0], got["r", dz, 0] = (w_rows(xm, z_of[dz], 0), plus), w_rows(x2, z_of[dz], 0)
        sent["r", dz, 1], got["r", dz, 1] = (w_rows(xp, z_of[dz], 1), minus), w_rows(x2, z_of[dz], 1)
    number = {name: n for n, name in enumerate(sent)}

    def w_copy(name, ref, to):
        n = number[name]
        return pltpu.make_async_remote_copy(
            src_ref=ref, dst_ref=ref, send_sem=w_send.at[n], recv_sem=w_recv.at[n],
            device_id=to, device_id_type=MESH,
        )

    seen = set()

    def w_start(*names):
        for name in names:
            w_copy(name, *sent[name]).start()

    def w_wait(*names):
        for name in names:
            seen.add(name)
            w_copy(name, got[name], plus).wait_recv()

    def both(dz, h):
        w_start(("x", dz, h, 0), ("x", dz, h, 1))

    def relay(dz):
        w_wait(("x", dz, 0, 0))
        w_start(("r", dz, 0))
        w_wait(("x", dz, 1, 1))
        w_start(("r", dz, 1))

    def step_a():
        w_wait(("z", 0, 0))
        both(1, 0)
        w_start(("y", 0))
        w_wait(("z", 0, 1))
        both(2, 0)

    def step_b():
        w_wait(("z", 1, 1))
        w_start(("y", 1))
        both(2, 1)
        w_wait(("z", 1, 0))
        both(1, 1)

    def step_c():
        w_wait(("y", 0))
        both(3, 0)
        w_wait(("y", 1))
        both(3, 1)

    def token_copy(slot, to):
        return pltpu.make_async_remote_copy(
            src_ref=tk.at[1], dst_ref=tk.at[slot], send_sem=t_send.at[slot // 2],
            recv_sem=t_recv.at[slot // 2], device_id={"ctx": to}, device_id_type=MESH,
        )

    def power_copy(d, ref):
        return pltpu.make_async_remote_copy(
            src_ref=ref, dst_ref=ref, send_sem=p_send.at[d - 1], recv_sem=p_recv.at[d - 1],
            device_id={"ch": lax.rem(ch + d, 4)}, device_id_type=MESH,
        )

    pl.semaphore_wait(barrier, 23)
    token_copy(0, after).start()
    token_copy(2, before).start()
    for d in range(1, 4):
        power_copy(d, pw.at[ch]).start()
    w_start(("z", 0, 0), ("z", 0, 1))
    both(0, 0)
    both(0, 1)
    w_start(("z", 1, 0), ("z", 1, 1))

    pick_rows(own_ids, own_other, (ext_f, rows), (ext_r, 0))
    first = me * rows
    pos = (iota((rows, segs), 0) + first).astype(f32)
    start_col = jnp.max(jnp.where(starts_row <= pos, starts_row, 0.0), axis=1, keepdims=True)
    end_col = jnp.min(jnp.where(ends_row > pos, ends_row, 1e9), axis=1, keepdims=True)
    start_col = jnp.broadcast_to(start_col, (rows, LANES)).astype(jnp.int32) - first
    end_col = jnp.broadcast_to(end_col, (rows, LANES)).astype(jnp.int32) - first
    for s in range(SUB):
        sv[pl.ds(s, rows, stride=SUB), :] = start_col
        ev[pl.ds(s, rows, stride=SUB), :] = end_col
    fetch[2].wait()
    prep_taps(taps_ref, tv, dv, tr, dr)

    token_copy(0, after).wait_recv()
    token_copy(2, before).wait_recv()
    last_ids = ids_of(0)
    next_other = other_of(ids_of(2))
    pick_rows(last_ids, next_other, (ext_f, 0), (ext_r, rows))

    for d in range(1, 4):
        power_copy(d, pw.at[lax.rem(ch + 4 - d, 4)]).wait_recv()
    power = (pw[0] + pw[1]) + (pw[2] + pw[3])
    inv_row = lax.rsqrt(power / (4 * width) + norm_eps)[0:1]
    for ref, at, ids in (
        (inv_f, 0, last_ids), (inv_f, rows, own_ids), (inv_r, 0, own_other), (inv_r, rows, next_other),
    ):
        col = jnp.sum(jnp.where(letters == ids, inv_row, 0.0), axis=1, keepdims=True)
        col = jnp.broadcast_to(col, (rows, LANES))
        for s in range(SUB):
            ref[pl.ds(at * SUB + s, rows, stride=SUB), :] = col

    def scale_rows(i, carry):
        for ext, inv in ((ext_f, inv_f), (ext_r, inv_r)):
            value = rows3(ext, i * 16, 16) * rows3(inv, i * 16, 16) * gain8[...][None]
            put3(ext, i * 16, value.astype(bf16).astype(f32))
        return carry

    lax.fori_loop(0, 2 * rows // 16, scale_rows, 0)
    relay(0)

    chunk = 16
    parts = rows // chunk
    direct = parts - 2

    def s_rows(cy, k):
        return sbuf.at[pl.ds(pl.multiple_of(cy * rows + k * chunk, chunk), chunk), :]

    def s_copy(k, kind, ref, cy):
        return pltpu.make_async_remote_copy(
            src_ref=ref, dst_ref=ref, send_sem=s_send.at[3 * k + kind],
            recv_sem=s_recv.at[3 * k + kind], device_id=at_ctx(x, zh, cy), device_id_type=MESH,
        )

    def s_relay(k):
        side = lax.rem(k, 2)
        there = s_rows(ring(y, 3 - 2 * side), k)
        s_copy(k, side, there, yp).wait_recv()
        s_copy(k, 2, there, ring(y, 1 + 2 * side)).start()

    steps = {0: step_a, 2: step_b, 3: lambda: relay(1), 4: step_c, 5: lambda: relay(2), 7: lambda: relay(3)}

    def sixteen(i, carry):
        conv_block(i, rows, ext_f, ext_r, tv, dv, tr, dr, sv, ev, res)
        at = pl.ds(pl.multiple_of(y * rows + i * chunk, chunk), chunk)
        for s in range(SUB):
            block = res[pl.ds(i * chunk * SUB + s, chunk, stride=SUB), :]
            sbuf[at, s * LANES : (s + 1) * LANES] = block.astype(bf16)
        s_copy(i, 0, s_rows(y, i), yp).start()
        s_copy(i, 1, s_rows(y, i), ym).start()

        @pl.when(i >= direct)
        def _():
            s_copy(i, 2, s_rows(y, i), y2).start()

        @pl.when(i >= 2)
        def _():
            s_relay(i - 2)

        for when, step in steps.items():
            pl.when(i == when)(step)
        return carry

    lax.fori_loop(0, parts, sixteen, 0)

    blocks = owner_ref.shape[1]
    spread = ((iota((blocks, segs), 1) >> 2) == iota((blocks, segs), 0)).astype(bf16)
    owners = jnp.broadcast_to(owner_ref[...], (SUB, blocks)).astype(f32).astype(bf16)
    owner_row = jnp.dot(owners, spread, preferred_element_type=f32)[0:1].astype(jnp.int32)
    slot, seg = iota((segs, segs), 0), iota((segs, segs), 1)
    same = (owner_row == (slot >> 2)) & ((slot & 3) == (seg & 3))
    slot_start = jnp.sum(jnp.where(same, starts_row, 0.0), axis=1, keepdims=True)
    slot_end = jnp.sum(jnp.where(same, ends_row, 0.0), axis=1, keepdims=True)
    total = 4 * rows
    spot = (iota((segs, total), 1) + lax.div(me, 4) * total).astype(f32)
    member[...] = ((slot_start <= spot) & (spot < slot_end)).astype(f32).astype(bf16)
    scale[...] = jnp.broadcast_to(slot_end - slot_start, (segs, LANES))

    def s_finish(k, carry):
        side = lax.rem(k, 2)
        s_copy(k, 1 - side, s_rows(ring(y, 1 + 2 * side), k), yp).wait_recv()
        s_copy(k, 2, s_rows(y2, k), yp).wait_recv()

        @pl.when(k >= direct)
        def _():
            s_copy(k, side, s_rows(ring(y, 3 - 2 * side), k), yp).wait_recv()

        return carry

    lax.fori_loop(0, parts, s_finish, 0)
    w_wait(*[name for name in got if name not in seen])

    group = 4 * cols

    def product(g):
        rhs = wbuf[pl.ds(pl.multiple_of(g * group, group), group), :]
        return lax.dot_general(
            sbuf[...], rhs, (((1,), (1,)), ((), ())), preferred_element_type=f32
        )

    def core_copy(n):
        return pltpu.make_async_remote_copy(
            src_ref=out1.at[n], dst_ref=in1.at[n], send_sem=r_send.at[n],
            recv_sem=r_recv.at[n], device_id={"ch": core_peer}, device_id_type=MESH,
        )

    def z_copy(t):
        at = pl.ds(t * rows, rows)
        return pltpu.make_async_remote_copy(
            src_ref=zout.at[at, :], dst_ref=zin.at[at, :], send_sem=z_send.at[t],
            recv_sem=z_recv.at[t], device_id={"ch": z_peer}, device_id_type=MESH,
        )

    out1[0] = product(2 * (1 - zl) + 1 - core).astype(bf16)
    core_copy(0).start()
    kept[...] = product(2 * (1 - zl) + core)
    core_copy(0).wait_recv()
    for t in range(4):
        at = pl.ds(t * rows, rows)
        zout[at, :] = (kept[at, :] + in1[0, at, :].astype(f32)).astype(bf16)
        z_copy(t).start()
    out1[1] = product(2 * zl + 1 - core).astype(bf16)
    core_copy(1).start()
    kept[...] = product(2 * zl + core)
    core_copy(1).wait_recv()

    sums = jnp.zeros((segs, group), f32)
    for t in range(4):
        at = pl.ds(t * rows, rows)
        z_copy(t).wait_recv()
        scores = kept[at, :] + in1[1, at, :].astype(f32) + zin[at, :].astype(f32)
        active = jnp.maximum(scores, 0.0) + jnp.log1p(jnp.exp(-jnp.abs(scores)))
        high = active.astype(bf16)
        low = (active - high.astype(f32)).astype(bf16)
        picks = member[:, t * rows : (t + 1) * rows]
        sums = sums + jnp.dot(picks, high, preferred_element_type=f32)
        sums = sums + jnp.dot(picks, low, preferred_element_type=f32)
    wide = group // LANES
    for h in range(wide):
        pbuf[pl.ds(h, segs, stride=wide), :] = sums[:, h * LANES : (h + 1) * LANES] / scale[...]

    share = 16 * SUB

    def to_x(d):
        return pltpu.make_async_remote_copy(
            src_ref=pbuf.at[pl.ds(pl.multiple_of(ring(x, d) * share, share), share), :],
            dst_ref=xbuf.at[d - 1], send_sem=x_send.at[d - 1], recv_sem=x_recv.at[d - 1],
            device_id=at_ctx(ring(x, d), zh, y), device_id_type=MESH,
        )

    for d in range(1, 4):
        to_x(d).start()
    mine = pbuf[pl.ds(pl.multiple_of(x * share, share), share), :]
    for d in range(1, 4):
        to_x(d).wait_recv()
        mine = mine + xbuf[d - 1]
    abuf[...] = mine

    def tile_at(cz, cy):
        return pl.ds(pl.multiple_of((cz * 4 + cy) * SUB, SUB), SUB)

    def to_owner(d, carry):
        cz, cy = ring(zh, lax.div(d, 4)), ring(y, lax.rem(d, 4))
        pltpu.make_async_remote_copy(
            src_ref=abuf.at[tile_at(cz, cy), :], dst_ref=rbuf.at[tile_at(zh, y), :],
            send_sem=a_send, recv_sem=a_recv, device_id=plane(d), device_id_type=MESH,
        ).start()
        return carry

    lax.fori_loop(1, 16, to_owner, 0)
    rbuf[tile_at(zh, y), :] = abuf[tile_at(zh, y), :]
    most = pl.ds(0, 15 * SUB)
    all_of = pltpu.make_async_remote_copy(
        src_ref=abuf.at[most, :], dst_ref=rbuf.at[most, :], send_sem=a_send, recv_sem=a_recv,
        device_id=plane(1), device_id_type=MESH,
    )
    all_of.wait_recv()
    for q in range(4):
        acc = rbuf[pl.ds(q * SUB, SUB), :]
        for m in range(1, 4):
            acc = acc + rbuf[pl.ds((4 * m + q) * SUB, SUB), :]
        obuf[pl.ds(q * SUB, SUB), :] = acc
        obuf[pl.ds((4 + q) * SUB, SUB), :] = pltpu.roll(acc, LANES // 2, 1)
    count = out_ref.shape[0]
    left = iota((count, LANES), 1) < LANES // 2
    for hz in range(2):
        for q in range(2):
            plain = [obuf[pl.ds((2 * q + n) * SUB + hz, count, stride=2), :] for n in range(2)]
            moved = [obuf[pl.ds((4 + 2 * q + n) * SUB + hz, count, stride=2), :] for n in range(2)]
            for b in range(2):
                pair = (plain[0], moved[1]) if b == 0 else (moved[0], plain[1])
                lane = ((2 * hz + b) * 2 + q) * LANES
                out_ref[:, lane : lane + LANES] = jnp.where(left, *pair)

    all_of.wait_send()
    for name in sent:
        w_copy(name, *sent[name]).wait_send()

    def s_drain(k, carry):
        for kind in range(3):
            s_copy(k, kind, s_rows(y, k), yp).wait_send()
        return carry

    lax.fori_loop(0, parts, s_drain, 0)
    for d in range(1, 4):
        power_copy(d, pw.at[ch]).wait_send()
        to_x(d).wait_send()
    token_copy(0, after).wait_send()
    token_copy(2, before).wait_send()
    core_copy(0).wait_send()
    core_copy(1).wait_send()
    for t in range(4):
        z_copy(t).wait_send()


def body(tokens, complement, seg_lengths, owner, embed, norm_gain, taps, w_out):
    rows = tokens.shape[0]
    vocab, width = embed.shape
    cols = w_out.shape[1]
    segs = seg_lengths.shape[0]
    per_block = segs // owner.shape[0]
    total, group = 4 * rows, 4 * cols
    vmem = pl.BlockSpec(memory_space=pltpu.VMEM)
    hbm = pl.BlockSpec(memory_space=pl.ANY)

    def tiles(count, dtype=f32):
        return pltpu.VMEM((count * SUB, LANES), dtype)

    def sems(count):
        return pltpu.SemaphoreType.DMA((count,))

    return pl.pallas_call(
        score_kernel,
        out_shape=jax.ShapeDtypeStruct((per_block, width), f32),
        in_specs=[vmem] * 5 + [hbm] * 3,
        out_specs=vmem,
        scratch_shapes=[
            pltpu.VMEM((vocab, width), bf16),
            pltpu.VMEM((taps.shape[0], width), f32),
            pltpu.VMEM((total, width), bf16),
            pltpu.VMEM((16 * cols, width), bf16),
            pltpu.VMEM((2, total, group), bf16),
            pltpu.VMEM((2, total, group), bf16),
            pltpu.VMEM((total, group), bf16),
            pltpu.VMEM((total, group), bf16),
            pltpu.VMEM((total, group), f32),
            tiles(64),
            pltpu.VMEM((3, 16 * SUB, LANES), f32),
            tiles(16),
            tiles(16),
            tiles(8),
            pltpu.VMEM((segs, total), bf16),
            pltpu.VMEM((segs, LANES), f32),
            pltpu.VMEM((3, SUB, rows), jnp.int32),
            pltpu.VMEM((4, SUB, vocab), f32),
            tiles(1),
        ]
        + [tiles(2 * rows)] * 4
        + [tiles(TAPROWS)] * 4
        + [tiles(rows, jnp.int32)] * 2
        + [tiles(rows)]
        + [sems(3), sems(30), sems(30), sems(24), sems(24), sems(2), sems(2), sems(4), sems(4)]
        + [sems(3), sems(3), pltpu.SemaphoreType.DMA, pltpu.SemaphoreType.DMA]
        + [sems(2), sems(2), sems(3), sems(3)],
        compiler_params=pltpu.CompilerParams(
            vmem_limit_bytes=56 << 20, collective_id=0, has_side_effects=True
        ),
    )(
        tokens[None, :], complement[None, :], seg_lengths[None, :], owner[None, :],
        norm_gain[None, :], embed, taps, w_out.T,
    )


def solution(mesh):
    in_specs = (P("ctx"), P(), P(), P(), P(None, "ch"), P("ch"), P(None, "ch"), P("ch", "ctx"))
    out_specs = P("ctx", "ch")
    return jax.shard_map(body, mesh=mesh, in_specs=in_specs, out_specs=out_specs, check_vma=False)
```

time: 67.2 us -> 63.9 us (0.951)
  Pallas kernels: 65.4 us -> 62.4 us
    pallas_call x1, Pallas kernels: 65.4 us -> 62.4 us  [body(): pl.pallas_call(score_kernel, out_shape=jax.ShapeDtypeStruct((per_block, w...]
    reshape x2 -> x0, local copies, waits for them, and re-layouts: 1.49 us -> none  [the longest x1 0.8 us: body(): sums = sums.reshape(4, per_block, 4, cols)]
    unnamed x0 -> x1, local copies, waits for them, and re-layouts: none -> 1.32 us
where the time goes in v3:
time: 63.9 us; the launch traced here: 63.7 us
  Pallas kernels  62.4 us (98%)
  local copies, waits for them, and re-layouts  1.32 us (2%)
    pallas_call x1, Pallas kernels, body(): pl.pallas_call(score_kernel, out_shape=jax.ShapeDtypeStruct((per_block, w...  62.4 us
    unnamed x1, local copies, waits for them, and re-layouts  1.32 us

profile of v3, /device:TPU:1, one launch (start us, length us, event | category | flops | bytes accessed | tf_op | source)
XLA Modules:
  0.0 63.7 jit_solution(6224460341814669242)
XLA Ops:
  0.0 62.4 %shard_map.82 = f32[4,1024]{1,0:T(4,128)} custom-call(s32[1,128]{1,0:T(1,128)} %bitcast.10, s32[1,512]{1,0:T(1,128)} %bitcast.8, s32[1,256]{1,0:T(1,128)} %bitcast.9, s32[1,64]{1,0:T(1,128)} %bitcast.11, f32[1,1024]{1,0:T(1,128)} %bitcast.7, bf16[512,1024]{1,0:T(8,128)(2,1)} %embed_hbm.1, f32[128,1024]{1,0:T(8,128)} %taps_hbm.1, bf16[64,1024]{1,0:T(8,128)(2,1)} %bitcast.6), custom_call_target="tpu_custom_call" | custom-call | tf_op jit(solution)/shard_map/pallas_call | solution.py:572
  62.4 1.3 %copy.10 = f32[4,1024]{1,0:T(4,128)} copy(f32[4,1024]{1,0:T(4,128)} %shard_map.82) | data formatting | bytes 32768

commit v4 on v3

--- a/solution.py
+++ b/solution.py
@@ -361,7 +361,6 @@
 
     chunk = 16
     parts = rows // chunk
-    direct = parts - 2
 
     def s_rows(cy, k):
         return sbuf.at[pl.ds(pl.multiple_of(cy * rows + k * chunk, chunk), chunk), :]
@@ -372,13 +371,7 @@
             recv_sem=s_recv.at[3 * k + kind], device_id=at_ctx(x, zh, cy), device_id_type=MESH,
         )
 
-    def s_relay(k):
-        side = lax.rem(k, 2)
-        there = s_rows(ring(y, 3 - 2 * side), k)
-        s_copy(k, side, there, yp).wait_recv()
-        s_copy(k, 2, there, ring(y, 1 + 2 * side)).start()
-
-    steps = {0: step_a, 2: step_b, 3: lambda: relay(1), 4: step_c, 5: lambda: relay(2), 7: lambda: relay(3)}
+    steps = {1: step_a, 3: step_b, 5: step_c, 6: lambda: relay(2), 7: lambda: relay(1)}
 
     def sixteen(i, carry):
         conv_block(i, rows, ext_f, ext_r, tv, dv, tr, dr, sv, ev, res)
@@ -389,14 +382,7 @@
         s_copy(i, 0, s_rows(y, i), yp).start()
         s_copy(i, 1, s_rows(y, i), ym).start()
 
-        @pl.when(i >= direct)
-        def _():
-            s_copy(i, 2, s_rows(y, i), y2).start()
-
-        @pl.when(i >= 2)
-        def _():
-            s_relay(i - 2)
-
+        s_copy(i, 2, s_rows(y, i), y2).start()
         for when, step in steps.items():
             pl.when(i == when)(step)
         return carry
@@ -416,15 +402,11 @@
     member[...] = ((slot_start <= spot) & (spot < slot_end)).astype(f32).astype(bf16)
     scale[...] = jnp.broadcast_to(slot_end - slot_start, (segs, LANES))
 
+    relay(3)
+
     def s_finish(k, carry):
-        side = lax.rem(k, 2)
-        s_copy(k, 1 - side, s_rows(ring(y, 1 + 2 * side), k), yp).wait_recv()
-        s_copy(k, 2, s_rows(y2, k), yp).wait_recv()
-
-        @pl.when(k >= direct)
-        def _():
-            s_copy(k, side, s_rows(ring(y, 3 - 2 * side), k), yp).wait_recv()
-
+        for kind, cy in enumerate((ym, yp, y2)):
+            s_copy(k, kind, s_rows(cy, k), yp).wait_recv()
         return carry
 
     lax.fori_loop(0, parts, s_finish, 0)
@@ -444,57 +426,61 @@
             recv_sem=r_recv.at[n], device_id={"ch": core_peer}, device_id_type=MESH,
         )
 
-    def z_copy(t):
-        at = pl.ds(t * rows, rows)
+    def z_copy(h, t):
+        at = pl.ds(t * 2 * rows, 2 * rows)
         return pltpu.make_async_remote_copy(
-            src_ref=zout.at[at, :], dst_ref=zin.at[at, :], send_sem=z_send.at[t],
-            recv_sem=z_recv.at[t], device_id={"ch": z_peer}, device_id_type=MESH,
+            src_ref=zout.at[h, at, :], dst_ref=zin.at[h, at, :], send_sem=z_send.at[2 * h + t],
+            recv_sem=z_recv.at[2 * h + t], device_id={"ch": z_peer}, device_id_type=MESH,
         )
 
     out1[0] = product(2 * (1 - zl) + 1 - core).astype(bf16)
     core_copy(0).start()
     kept[...] = product(2 * (1 - zl) + core)
     core_copy(0).wait_recv()
-    for t in range(4):
-        at = pl.ds(t * rows, rows)
-        zout[at, :] = (kept[at, :] + in1[0, at, :].astype(f32)).astype(bf16)
-        z_copy(t).start()
+    for h in range(2):
+        lanes = slice(h * LANES, (h + 1) * LANES)
+        for t in range(2):
+            at = pl.ds(t * 2 * rows, 2 * rows)
+            zout[h, at, :] = (kept[at, lanes] + in1[0, at, lanes].astype(f32)).astype(bf16)
+            z_copy(h, t).start()
     out1[1] = product(2 * zl + 1 - core).astype(bf16)
     core_copy(1).start()
     kept[...] = product(2 * zl + core)
     core_copy(1).wait_recv()
 
-    sums = jnp.zeros((segs, group), f32)
-    for t in range(4):
-        at = pl.ds(t * rows, rows)
-        z_copy(t).wait_recv()
-        scores = kept[at, :] + in1[1, at, :].astype(f32) + zin[at, :].astype(f32)
-        active = jnp.maximum(scores, 0.0) + jnp.log1p(jnp.exp(-jnp.abs(scores)))
-        high = active.astype(bf16)
-        low = (active - high.astype(f32)).astype(bf16)
-        picks = member[:, t * rows : (t + 1) * rows]
-        sums = sums + jnp.dot(picks, high, preferred_element_type=f32)
-        sums = sums + jnp.dot(picks, low, preferred_element_type=f32)
-    wide = group // LANES
-    for h in range(wide):
-        pbuf[pl.ds(h, segs, stride=wide), :] = sums[:, h * LANES : (h + 1) * LANES] / scale[...]
-
-    share = 16 * SUB
-
-    def to_x(d):
+    share = 16 * SUB // 2
+
+    def to_x(h, d):
+        n = 3 * h + d - 1
         return pltpu.make_async_remote_copy(
-            src_ref=pbuf.at[pl.ds(pl.multiple_of(ring(x, d) * share, share), share), :],
-            dst_ref=xbuf.at[d - 1], send_sem=x_send.at[d - 1], recv_sem=x_recv.at[d - 1],
+            src_ref=pbuf.at[h, pl.ds(pl.multiple_of(ring(x, d) * share, share), share), :],
+            dst_ref=xbuf.at[n], send_sem=x_send.at[n], recv_sem=x_recv.at[n],
             device_id=at_ctx(ring(x, d), zh, y), device_id_type=MESH,
         )
 
-    for d in range(1, 4):
-        to_x(d).start()
-    mine = pbuf[pl.ds(pl.multiple_of(x * share, share), share), :]
-    for d in range(1, 4):
-        to_x(d).wait_recv()
-        mine = mine + xbuf[d - 1]
-    abuf[...] = mine
+    for h in range(2):
+        lanes = slice(h * LANES, (h + 1) * LANES)
+        highs, lows = [], []
+        for t in range(2):
+            at = pl.ds(t * 2 * rows, 2 * rows)
+            z_copy(h, t).wait_recv()
+            scores = kept[at, lanes] + in1[1, at, lanes].astype(f32) + zin[h, at, :].astype(f32)
+            active = jnp.maximum(scores, 0.0) + jnp.log1p(jnp.exp(-jnp.abs(scores)))
+            highs.append(active.astype(bf16))
+            lows.append((active - highs[-1].astype(f32)).astype(bf16))
+        halves = jnp.concatenate(
+            [jnp.concatenate(highs, axis=0), jnp.concatenate(lows, axis=0)], axis=1
+        )
+        sums = jnp.dot(member[...], halves, preferred_element_type=f32)
+        pbuf[h] = (sums[:, :LANES] + sums[:, LANES:]) / scale[...]
+        for d in range(1, 4):
+            to_x(h, d).start()
+    for h in range(2):
+        mine = pbuf[h, pl.ds(pl.multiple_of(x * share, share), share), :]
+        for d in range(1, 4):
+            to_x(h, d).wait_recv()
+            mine = mine + xbuf[3 * h + d - 1]
+        abuf[pl.ds(h, share, stride=2), :] = mine
 
     def tile_at(cz, cy):
         return pl.ds(pl.multiple_of((cz * 4 + cy) * SUB, SUB), SUB)
@@ -544,13 +530,14 @@
     lax.fori_loop(0, parts, s_drain, 0)
     for d in range(1, 4):
         power_copy(d, pw.at[ch]).wait_send()
-        to_x(d).wait_send()
+        to_x(0, d).wait_send()
+        to_x(1, d).wait_send()
     token_copy(0, after).wait_send()
     token_copy(2, before).wait_send()
     core_copy(0).wait_send()
     core_copy(1).wait_send()
-    for t in range(4):
-        z_copy(t).wait_send()
+    for n in range(4):
+        z_copy(n // 2, n % 2).wait_send()
 
 
 def body(tokens, complement, seg_lengths, owner, embed, norm_gain, taps, w_out):
@@ -581,11 +568,11 @@
             pltpu.VMEM((16 * cols, width), bf16),
             pltpu.VMEM((2, total, group), bf16),
             pltpu.VMEM((2, total, group), bf16),
-            pltpu.VMEM((total, group), bf16),
-            pltpu.VMEM((total, group), bf16),
+            pltpu.VMEM((2, total, LANES), bf16),
+            pltpu.VMEM((2, total, LANES), bf16),
             pltpu.VMEM((total, group), f32),
-            tiles(64),
-            pltpu.VMEM((3, 16 * SUB, LANES), f32),
+            pltpu.VMEM((2, segs, LANES), f32),
+            pltpu.VMEM((6, 8 * SUB, LANES), f32),
             tiles(16),
             tiles(16),
             tiles(8),
@@ -600,7 +587,7 @@
         + [tiles(rows, jnp.int32)] * 2
         + [tiles(rows)]
         + [sems(3), sems(30), sems(30), sems(24), sems(24), sems(2), sems(2), sems(4), sems(4)]
-        + [sems(3), sems(3), pltpu.SemaphoreType.DMA, pltpu.SemaphoreType.DMA]
+        + [sems(6), sems(6), pltpu.SemaphoreType.DMA, pltpu.SemaphoreType.DMA]
         + [sems(2), sems(2), sems(3), sems(3)],
         compiler_params=pltpu.CompilerParams(
             vmem_limit_bytes=56 << 20, collective_id=0, has_side_effects=True

time: 63.9 us -> 60.2 us (0.942)
  Pallas kernels: 62.4 us -> 58.7 us
    pallas_call x1, Pallas kernels: 62.4 us -> 58.7 us  [body(): pl.pallas_call(score_kernel, out_shape=jax.ShapeDtypeStruct((per_block, w...]
where the time goes in v4:
time: 60.2 us; the launch traced here: 60 us
  Pallas kernels  58.7 us (98%)
  local copies, waits for them, and re-layouts  1.32 us (2%)
    pallas_call x1, Pallas kernels, body(): pl.pallas_call(score_kernel, out_shape=jax.ShapeDtypeStruct((per_block, w...  58.7 us
    unnamed x1, local copies, waits for them, and re-layouts  1.32 us

profile of v4, /device:TPU:1, one launch (start us, length us, event | category | flops | bytes accessed | tf_op | source)
XLA Modules:
  0.0 60.0 jit_solution(15973419725997144778)
XLA Ops:
  0.0 58.7 %shard_map.82 = f32[4,1024]{1,0:T(4,128)} custom-call(s32[1,128]{1,0:T(1,128)} %bitcast.10, s32[1,512]{1,0:T(1,128)} %bitcast.8, s32[1,256]{1,0:T(1,128)} %bitcast.9, s32[1,64]{1,0:T(1,128)} %bitcast.11, f32[1,1024]{1,0:T(1,128)} %bitcast.7, bf16[512,1024]{1,0:T(8,128)(2,1)} %embed_hbm.1, f32[128,1024]{1,0:T(8,128)} %taps_hbm.1, bf16[64,1024]{1,0:T(8,128)(2,1)} %bitcast.6), custom_call_target="tpu_custom_call" | custom-call | tf_op jit(solution)/shard_map/pallas_call | solution.py:559
  58.7 1.3 %copy.10 = f32[4,1024]{1,0:T(4,128)} copy(f32[4,1024]{1,0:T(4,128)} %shard_map.82) | data formatting | bytes 32768

commit v5 on v4

--- a/solution.py
+++ b/solution.py
@@ -77,10 +77,28 @@
             c = c + rows3(dr, BASE - 8 - lag - u, 8) * x1[u:u + 1]
         return a, b, c
 
-    a, b, c = lax.fori_loop(1, far_lags + 1, fwd_far, (zero8,) * 3, unroll=2)
-    far_f = (a + b, a - c)
-    a, b, c = lax.fori_loop(1, far_lags + 1, rev_far, (zero8,) * 3, unroll=2)
-    far_r = (a - c, a + b)
+    def part(value, lo, term):
+        pieces = [value[:lo], value[lo : lo + term.shape[0]] + term, value[lo + term.shape[0] :]]
+        return jnp.concatenate([piece for piece in pieces if piece.shape[0]], axis=0)
+
+    a, b, c = lax.fori_loop(1, far_lags, fwd_far, (zero8,) * 3, unroll=7)
+    far_f = [a + b, a - c]
+    rows = jnp.where(idx16 >= s0 - (p0 - SPAN), rows3(ext_f, count + p0 - SPAN, 16), 0.0)
+    for u in range(8):
+        far_f[0] = far_f[0] + rows3(tv, PAD + SPAN - 8 - u, 8) * rows[8 + u : 9 + u]
+        if u:
+            tap = rows3(tv, PAD + SPAN - u, u)
+            far_f[0] = part(far_f[0], 0, tap * rows[u : u + 1])
+            far_f[1] = part(far_f[1], 0, tap * rows[8 + u : 9 + u])
+    a, b, c = lax.fori_loop(1, far_lags, rev_far, (zero8,) * 3, unroll=7)
+    far_r = [a - c, a + b]
+    rows = jnp.where(idx16 < e0 - (p0 + SPAN), rows3(ext_r, p0 + SPAN, 16), 0.0)
+    for u in range(8):
+        far_r[1] = far_r[1] + rows3(tr, BASE - SPAN + 8 - u, 8) * rows[u : u + 1]
+        if u < 7:
+            tap = rows3(tr, BASE - SPAN + 1, 7 - u)
+            far_r[0] = part(far_r[0], u + 1, tap * rows[u : u + 1])
+            far_r[1] = part(far_r[1], u + 1, tap * rows[8 + u : 9 + u])
     xf = (rows3(ext_f, count + p0, 8), rows3(ext_f, count + p0 + 8, 8))
     xr = (rows3(ext_r, p0, 8), rows3(ext_r, p0 + 8, 8))
     idx8 = lax.broadcasted_iota(jnp.int32, (8, SUB, LANES), 0)
@@ -371,7 +389,7 @@
             recv_sem=s_recv.at[3 * k + kind], device_id=at_ctx(x, zh, cy), device_id_type=MESH,
         )
 
-    steps = {1: step_a, 3: step_b, 5: step_c, 6: lambda: relay(2), 7: lambda: relay(1)}
+    steps = {0: step_a, 2: step_b, 4: step_c, 6: lambda: relay(2), 7: lambda: relay(1)}
 
     def sixteen(i, carry):
         conv_block(i, rows, ext_f, ext_r, tv, dv, tr, dr, sv, ev, res)
@@ -414,8 +432,8 @@
 
     group = 4 * cols
 
-    def product(g):
-        rhs = wbuf[pl.ds(pl.multiple_of(g * group, group), group), :]
+    def product(g, h):
+        rhs = wbuf[pl.ds(pl.multiple_of(g * group + h * LANES, LANES), LANES), :]
         return lax.dot_general(
             sbuf[...], rhs, (((1,), (1,)), ((), ())), preferred_element_type=f32
         )
@@ -433,20 +451,21 @@
             recv_sem=z_recv.at[2 * h + t], device_id={"ch": z_peer}, device_id_type=MESH,
         )
 
-    out1[0] = product(2 * (1 - zl) + 1 - core).astype(bf16)
-    core_copy(0).start()
-    kept[...] = product(2 * (1 - zl) + core)
-    core_copy(0).wait_recv()
-    for h in range(2):
-        lanes = slice(h * LANES, (h + 1) * LANES)
+    for h in range(2):
+        out1[h] = product(2 * (1 - zl) + 1 - core, h).astype(bf16)
+        core_copy(h).start()
+    for h in range(2):
+        kept[h] = product(2 * (1 - zl) + core, h)
+        core_copy(h).wait_recv()
         for t in range(2):
             at = pl.ds(t * 2 * rows, 2 * rows)
-            zout[h, at, :] = (kept[at, lanes] + in1[0, at, lanes].astype(f32)).astype(bf16)
+            zout[h, at, :] = (kept[h, at, :] + in1[h, at, :].astype(f32)).astype(bf16)
             z_copy(h, t).start()
-    out1[1] = product(2 * zl + 1 - core).astype(bf16)
-    core_copy(1).start()
-    kept[...] = product(2 * zl + core)
-    core_copy(1).wait_recv()
+    for h in range(2):
+        out1[2 + h] = product(2 * zl + 1 - core, h).astype(bf16)
+        core_copy(2 + h).start()
+    for h in range(2):
+        kept[h] = product(2 * zl + core, h)
 
     share = 16 * SUB // 2
 
@@ -459,12 +478,12 @@
         )
 
     for h in range(2):
-        lanes = slice(h * LANES, (h + 1) * LANES)
         highs, lows = [], []
+        core_copy(2 + h).wait_recv()
         for t in range(2):
             at = pl.ds(t * 2 * rows, 2 * rows)
             z_copy(h, t).wait_recv()
-            scores = kept[at, lanes] + in1[1, at, lanes].astype(f32) + zin[h, at, :].astype(f32)
+            scores = kept[h, at, :] + in1[2 + h, at, :].astype(f32) + zin[h, at, :].astype(f32)
             active = jnp.maximum(scores, 0.0) + jnp.log1p(jnp.exp(-jnp.abs(scores)))
             highs.append(active.astype(bf16))
             lows.append((active - highs[-1].astype(f32)).astype(bf16))
@@ -534,9 +553,8 @@
         to_x(1, d).wait_send()
     token_copy(0, after).wait_send()
     token_copy(2, before).wait_send()
-    core_copy(0).wait_send()
-    core_copy(1).wait_send()
     for n in range(4):
+        core_copy(n).wait_send()
         z_copy(n // 2, n % 2).wait_send()
 
 
@@ -566,11 +584,11 @@
             pltpu.VMEM((taps.shape[0], width), f32),
             pltpu.VMEM((total, width), bf16),
             pltpu.VMEM((16 * cols, width), bf16),
-            pltpu.VMEM((2, total, group), bf16),
-            pltpu.VMEM((2, total, group), bf16),
+            pltpu.VMEM((4, total, LANES), bf16),
+            pltpu.VMEM((4, total, LANES), bf16),
             pltpu.VMEM((2, total, LANES), bf16),
             pltpu.VMEM((2, total, LANES), bf16),
-            pltpu.VMEM((total, group), f32),
+            pltpu.VMEM((2, total, LANES), f32),
             pltpu.VMEM((2, segs, LANES), f32),
             pltpu.VMEM((6, 8 * SUB, LANES), f32),
             tiles(16),
@@ -586,7 +604,7 @@
         + [tiles(TAPROWS)] * 4
         + [tiles(rows, jnp.int32)] * 2
         + [tiles(rows)]
-        + [sems(3), sems(30), sems(30), sems(24), sems(24), sems(2), sems(2), sems(4), sems(4)]
+        + [sems(3), sems(30), sems(30), sems(24), sems(24), sems(4), sems(4), sems(4), sems(4)]
         + [sems(6), sems(6), pltpu.SemaphoreType.DMA, pltpu.SemaphoreType.DMA]
         + [sems(2), sems(2), sems(3), sems(3)],
         compiler_params=pltpu.CompilerParams(

time: 60.2 us -> 58.6 us (0.973)
  Pallas kernels: 58.7 us -> 56.7 us
    pallas_call x1, Pallas kernels: 58.7 us -> 56.7 us  [body(): pl.pallas_call(score_kernel, out_shape=jax.ShapeDtypeStruct((per_block, w...]
where the time goes in v5:
time: 58.6 us; the launch traced here: 58 us
  Pallas kernels  56.7 us (97%)
  local copies, waits for them, and re-layouts  1.32 us (2%)
    pallas_call x1, Pallas kernels, body(): pl.pallas_call(score_kernel, out_shape=jax.ShapeDtypeStruct((per_block, w...  56.7 us
    unnamed x1, local copies, waits for them, and re-layouts  1.32 us

profile of v5, /device:TPU:1, one launch (start us, length us, event | category | flops | bytes accessed | tf_op | source)
XLA Modules:
  0.0 58.0 jit_solution(5264802210478765739)
XLA Ops:
  0.0 56.7 %shard_map.82 = f32[4,1024]{1,0:T(4,128)} custom-call(s32[1,128]{1,0:T(1,128)} %bitcast.10, s32[1,512]{1,0:T(1,128)} %bitcast.8, s32[1,256]{1,0:T(1,128)} %bitcast.9, s32[1,64]{1,0:T(1,128)} %bitcast.11, f32[1,1024]{1,0:T(1,128)} %bitcast.7, bf16[512,1024]{1,0:T(8,128)(2,1)} %embed_hbm.1, f32[128,1024]{1,0:T(8,128)} %taps_hbm.1, bf16[64,1024]{1,0:T(8,128)(2,1)} %bitcast.6), custom_call_target="tpu_custom_call" | custom-call | tf_op jit(solution)/shard_map/pallas_call | solution.py:577
  56.7 1.3 %copy.10 = f32[4,1024]{1,0:T(4,128)} copy(f32[4,1024]{1,0:T(4,128)} %shard_map.82) | data formatting | bytes 32768

commit v6 on v5

--- a/solution.py
+++ b/solution.py
@@ -376,6 +376,7 @@
 
     lax.fori_loop(0, 2 * rows // 16, scale_rows, 0)
     relay(0)
+    step_a()
 
     chunk = 16
     parts = rows // chunk
@@ -389,7 +390,7 @@
             recv_sem=s_recv.at[3 * k + kind], device_id=at_ctx(x, zh, cy), device_id_type=MESH,
         )
 
-    steps = {0: step_a, 2: step_b, 4: step_c, 6: lambda: relay(2), 7: lambda: relay(1)}
+    steps = {1: step_b, 3: step_c, 5: lambda: relay(2), 6: lambda: relay(1), 7: lambda: relay(3)}
 
     def sixteen(i, carry):
         conv_block(i, rows, ext_f, ext_r, tv, dv, tr, dr, sv, ev, res)
@@ -397,10 +398,8 @@
         for s in range(SUB):
             block = res[pl.ds(i * chunk * SUB + s, chunk, stride=SUB), :]
             sbuf[at, s * LANES : (s + 1) * LANES] = block.astype(bf16)
-        s_copy(i, 0, s_rows(y, i), yp).start()
-        s_copy(i, 1, s_rows(y, i), ym).start()
-
-        s_copy(i, 2, s_rows(y, i), y2).start()
+        for kind, cy in ((2, y2), (0, yp), (1, ym)):
+            s_copy(i, kind, s_rows(y, i), cy).start()
         for when, step in steps.items():
             pl.when(i == when)(step)
         return carry
@@ -420,8 +419,6 @@
     member[...] = ((slot_start <= spot) & (spot < slot_end)).astype(f32).astype(bf16)
     scale[...] = jnp.broadcast_to(slot_end - slot_start, (segs, LANES))
 
-    relay(3)
-
     def s_finish(k, carry):
         for kind, cy in enumerate((ym, yp, y2)):
             s_copy(k, kind, s_rows(cy, k), yp).wait_recv()
@@ -492,7 +489,7 @@
         )
         sums = jnp.dot(member[...], halves, preferred_element_type=f32)
         pbuf[h] = (sums[:, :LANES] + sums[:, LANES:]) / scale[...]
-        for d in range(1, 4):
+        for d in (2, 1, 3):
             to_x(h, d).start()
     for h in range(2):
         mine = pbuf[h, pl.ds(pl.multiple_of(x * share, share), share), :]

time: 58.6 us -> 57.5 us (0.981)
  Pallas kernels: 56.7 us -> 56 us
    pallas_call x1, Pallas kernels: 56.7 us -> 56 us  [body(): pl.pallas_call(score_kernel, out_shape=jax.ShapeDtypeStruct((per_block, w...]
where the time goes in v6:
time: 57.5 us; the launch traced here: 57.3 us
  Pallas kernels  56 us (97%)
  local copies, waits for them, and re-layouts  1.32 us (2%)
    pallas_call x1, Pallas kernels, body(): pl.pallas_call(score_kernel, out_shape=jax.ShapeDtypeStruct((per_block, w...  56 us
    unnamed x1, local copies, waits for them, and re-layouts  1.32 us

profile of v6, /device:TPU:1, one launch (start us, length us, event | category | flops | bytes accessed | tf_op | source)
XLA Modules:
  0.0 57.3 jit_solution(7961383710947884481)
XLA Ops:
  0.0 56.0 %shard_map.82 = f32[4,1024]{1,0:T(4,128)} custom-call(s32[1,128]{1,0:T(1,128)} %bitcast.10, s32[1,512]{1,0:T(1,128)} %bitcast.8, s32[1,256]{1,0:T(1,128)} %bitcast.9, s32[1,64]{1,0:T(1,128)} %bitcast.11, f32[1,1024]{1,0:T(1,128)} %bitcast.7, bf16[512,1024]{1,0:T(8,128)(2,1)} %embed_hbm.1, f32[128,1024]{1,0:T(8,128)} %taps_hbm.1, bf16[64,1024]{1,0:T(8,128)(2,1)} %bitcast.6), custom_call_target="tpu_custom_call" | custom-call | tf_op jit(solution)/shard_map/pallas_call | solution.py:574
  56.0 1.3 %copy.10 = f32[4,1024]{1,0:T(4,128)} copy(f32[4,1024]{1,0:T(4,128)} %shard_map.82) | data formatting | bytes 32768

commit v7 on v6

--- a/solution.py
+++ b/solution.py
@@ -144,7 +144,7 @@
 
 def score_kernel(tok_ref, comp_ref, lens_ref, owner_ref, gain_ref, embed_hbm, taps_hbm, w_hbm,
                  out_ref, embed_ref, taps_ref, sbuf, wbuf, out1, in1, zout, zin, kept,
-                 pbuf, xbuf, abuf, rbuf, obuf, member, scale, tk, pw, gain8,
+                 pbuf, psend, xbuf, abuf, rbuf, obuf, member, scale, tk, pw, gain8,
                  ext_f, ext_r, inv_f, inv_r, tv, dv, tr, dr, sv, ev, res,
                  l_sem, w_send, w_recv, s_send, s_recv, r_send, r_recv, z_send, z_recv,
                  x_send, x_recv, a_send, a_recv, t_send, t_recv, p_send, p_recv):
@@ -469,7 +469,7 @@
     def to_x(h, d):
         n = 3 * h + d - 1
         return pltpu.make_async_remote_copy(
-            src_ref=pbuf.at[h, pl.ds(pl.multiple_of(ring(x, d) * share, share), share), :],
+            src_ref=psend.at[h, pl.ds(pl.multiple_of(ring(x, d) * share, share), share), :],
             dst_ref=xbuf.at[n], send_sem=x_send.at[n], recv_sem=x_recv.at[n],
             device_id=at_ctx(ring(x, d), zh, y), device_id_type=MESH,
         )
@@ -489,13 +489,14 @@
         )
         sums = jnp.dot(member[...], halves, preferred_element_type=f32)
         pbuf[h] = (sums[:, :LANES] + sums[:, LANES:]) / scale[...]
+        psend[h] = pbuf[h].astype(bf16)
         for d in (2, 1, 3):
             to_x(h, d).start()
     for h in range(2):
         mine = pbuf[h, pl.ds(pl.multiple_of(x * share, share), share), :]
         for d in range(1, 4):
             to_x(h, d).wait_recv()
-            mine = mine + xbuf[3 * h + d - 1]
+            mine = mine + xbuf[3 * h + d - 1].astype(f32)
         abuf[pl.ds(h, share, stride=2), :] = mine
 
     def tile_at(cz, cy):
@@ -587,7 +588,8 @@
             pltpu.VMEM((2, total, LANES), bf16),
             pltpu.VMEM((2, total, LANES), f32),
             pltpu.VMEM((2, segs, LANES), f32),
-            pltpu.VMEM((6, 8 * SUB, LANES), f32),
+            pltpu.VMEM((2, segs, LANES), bf16),
+            pltpu.VMEM((6, 8 * SUB, LANES), bf16),
             tiles(16),
             tiles(16),
             tiles(8),

time: 57.5 us -> 57.3 us (level)
  no operation moved by 1% of the time
where the time goes in v7:
time: 57.3 us; the launch traced here: 57.1 us
  Pallas kernels  55.8 us (97%)
  local copies, waits for them, and re-layouts  1.32 us (2%)
    pallas_call x1, Pallas kernels, body(): pl.pallas_call(score_kernel, out_shape=jax.ShapeDtypeStruct((per_block, w...  55.8 us
    unnamed x1, local copies, waits for them, and re-layouts  1.32 us

profile of v7, /device:TPU:1, one launch (start us, length us, event | category | flops | bytes accessed | tf_op | source)
XLA Modules:
  0.0 57.1 jit_solution(7436024674410374459)
XLA Ops:
  0.0 55.8 %shard_map.82 = f32[4,1024]{1,0:T(4,128)} custom-call(s32[1,128]{1,0:T(1,128)} %bitcast.10, s32[1,512]{1,0:T(1,128)} %bitcast.8, s32[1,256]{1,0:T(1,128)} %bitcast.9, s32[1,64]{1,0:T(1,128)} %bitcast.11, f32[1,1024]{1,0:T(1,128)} %bitcast.7, bf16[512,1024]{1,0:T(8,128)(2,1)} %embed_hbm.1, f32[128,1024]{1,0:T(8,128)} %taps_hbm.1, bf16[64,1024]{1,0:T(8,128)(2,1)} %bitcast.6), custom_call_target="tpu_custom_call" | custom-call | tf_op jit(solution)/shard_map/pallas_call | solution.py:575
  55.8 1.3 %copy.10 = f32[4,1024]{1,0:T(4,128)} copy(f32[4,1024]{1,0:T(4,128)} %shard_map.82) | data formatting | bytes 32768
